TPU v7x, 256 devices: a whole 4x4x8 slice. The times are simulated.
256 devices in a mesh: inner: 16 (over x, y), outer: 16 (over z, core).
Axes of the slice: x: 4, y: 4, z: 8, core: 2. Of those that a mesh axis runs over, the one named last changes fastest.
Arguments:
- jac: float32 [4096, 256, 256], P(('outer', 'inner')), may hold values from -0.5 to 1
- obs: float32 [4096, 256], P(('outer', 'inner')), may hold values from -6 to 6
- gain_filter: float32 [256], replicated, may hold values from 0 to 0.1
- gain_smooth: float32 [256, 256], replicated, may hold values from -0.5 to 1
- init_mean: float32 [256], replicated, may hold values from -6 to 6
Outputs:
- filtered: float32 [4096, 256], P(('outer', 'inner'))
- smoothed: float32 [4096, 256], P(('outer', 'inner'))
All inputs are finite; a program needn't handle non-finite values.
Results may differ from a plain program's by a relative error of at most 0.0003.
Values sent between devices are 32-bit elements; how exact they have to be, the bound alone decides.
No kernel may reach another device: no remote copies, remote signals or barrier semaphores. Data moves between devices by JAX's collectives and lax.ppermute only.
A program may use at most 64 MiB of HBM per device.

v0:
```python
import functools

import jax
import jax.numpy as jnp
from jax import lax
from jax.experimental import pallas as pl
from jax.experimental.pallas import tpu as pltpu
from jax.sharding import PartitionSpec as P

HIGHEST = lax.Precision.HIGHEST
F32 = jnp.float32
VMEM = pl.BlockSpec(memory_space=pltpu.VMEM)
SMEM = pl.BlockSpec(memory_space=pltpu.SMEM)
HBM = pl.BlockSpec(memory_space=pltpu.MemorySpace.HBM)
PAD = 8


def dot_nn(a, b):
    return lax.dot_general(
        a, b, (((1,), (0,)), ((), ())), precision=HIGHEST, preferred_element_type=F32
    )


def dot_nt(a, b):
    return lax.dot_general(
        a, b, (((1,), (1,)), ((), ())), precision=HIGHEST, preferred_element_type=F32
    )


def kernel_call(body, out_shape, in_specs, args, name, scratch=(), flops=0, size=0, grant=4, out_specs=None):
    many = isinstance(out_shape, list)
    shapes = [jax.ShapeDtypeStruct(s, F32) for s in (out_shape if many else [out_shape])]
    out = pl.pallas_call(
        body,
        out_shape=shapes,
        in_specs=in_specs,
        out_specs=out_specs or [VMEM] * len(shapes),
        scratch_shapes=list(scratch),
        cost_estimate=pl.CostEstimate(flops=flops, bytes_accessed=size, transcendentals=0),
        compiler_params=pltpu.CompilerParams(vmem_limit_bytes=grant << 20),
        name=name,
    )(*args)
    return out if many else out[0]


def local_map_body(inner, outer, jac_hbm, obs_hbm, gain_hbm, out, quarter, half, third, buf, obs, gain, chain, sems):
    steps, n, _ = buf.shape
    small = [(obs_hbm, obs, steps), (gain_hbm, gain, steps + 1)]
    for source, dest, k in small:
        pltpu.make_async_copy(source, dest, sems.at[k]).start()
    pairs = steps // 2
    order = [2 * c + i for i in range(2) for c in range(pairs)]
    for t in order:
        pltpu.make_async_copy(jac_hbm.at[t], buf.at[t], sems.at[t]).start()
    for source, dest, k in small:
        pltpu.make_async_copy(source, dest, sems.at[k]).wait()
    g = gain[...]
    retain = 1.0 - g
    for t in order:
        pltpu.make_async_copy(jac_hbm.at[t], buf.at[t], sems.at[t]).wait()
        c = t // 2
        offset = jnp.broadcast_to(g * obs[t : t + 1, :], (PAD, n))
        if t % 2 == 0:
            chain[c, :n] = buf[t].T * retain
            chain[c, n:] = offset
        else:
            moved = dot_nt(chain[c], buf[t]) * retain
            chain[c, :n] = moved[:n]
            chain[c, n:] = moved[n:] + offset
    kept = {(0, pairs): out, (0, pairs // 2): half}
    kept[(0, pairs // 4)] = quarter
    kept[(pairs // 2, 3 * pairs // 4)] = third
    width = 1
    while width < pairs:
        for c in range(0, pairs, 2 * width):
            moved = dot_nn(chain[c], chain[c + width, :n])
            later = chain[c + width, n:]
            span = (c, c + 2 * width)
            dest = kept.get(span, chain.at[c])
            dest[:n] = moved[:n]
            dest[n:] = moved[n:] + later
            if span in kept and 2 * width < pairs:
                chain[c] = dest[...]
        width *= 2


def local_map(place, jac, obs, gain):
    steps, n, _ = jac.shape
    return kernel_call(
        local_map_body,
        [(n + PAD, n)] * 4 + [(steps, n, n)],
        [SMEM, SMEM, HBM, HBM, HBM],
        (*place, jac, obs, gain),
        "local_map",
        scratch=[
            pltpu.VMEM((steps, n), F32),
            pltpu.VMEM((1, n), F32),
            pltpu.VMEM((steps // 2, n + PAD, n), F32),
            pltpu.SemaphoreType.DMA((steps + 2,)),
        ],
        flops=12 * steps * n**3,
        size=4 * steps * n * n,
        grant=47,
    )


def join(earlier, later, out):
    n = out.shape[1]
    moved = dot_nn(earlier[...], later[:n])
    out[:n] = moved[:n]
    out[n:] = moved[n:] + later[n:]


def late(inner, outer, level):
    index = inner if level < 4 else outer
    return jnp.bitwise_and(jnp.right_shift(index[0], level % 4), 1) == 1


def total_body(level, inner, outer, own, other, out):
    n = out.shape[1]
    is_late = late(inner, outer, level)
    earlier = jnp.where(is_late, other[...], own[...])
    later = jnp.where(is_late, own[...], other[...])
    moved = dot_nn(earlier, later[:n])
    out[:n] = moved[:n]
    out[n:] = moved[n:] + later[n:]


def total_call(level, place, a, b):
    n = a.shape[1]
    return kernel_call(
        functools.partial(total_body, level),
        a.shape,
        [SMEM, SMEM, VMEM, VMEM],
        (*place, a, b),
        "total",
        flops=12 * n**3,
        size=12 * n * n,
    )


def hop_body(stage, outer, first, arrived, group_map, out):
    n = out.shape[1]
    state = jnp.broadcast_to(first[...], (PAD, n))
    if stage == 1:
        state = jnp.where(jnp.right_shift(outer[0], 2) == 1, arrived[...], state)
    out[...] = dot_nn(state, group_map[:n]) + group_map[n:]


def hop(stage, place, first, arrived, group_map):
    n = group_map.shape[1]
    return kernel_call(
        functools.partial(hop_body, stage),
        (PAD, n),
        [SMEM] + [VMEM] * 3,
        (place[1], first, arrived, group_map),
        "hop",
        flops=96 * n * n,
        size=4 * n * n,
    )


def maps_body(first, *refs):
    if first:
        quarter, half, third, jac, obs, gain, smooth, pi, pairs, phi = refs[:10]
        later, moving = refs[10:]
    else:
        given, even, jac, obs, gain, base_powers, pi, offset_map = refs[:8]
        later, moving, pairs = refs[8:]
    n = jac.shape[1]
    size = n + PAD
    lanes = 4
    depth = jac.shape[0] // lanes
    if first:
        row = lax.broadcasted_iota(jnp.int32, (size, n), 0)
        column = lax.broadcasted_iota(jnp.int32, (size, n), 1)
        moving[0] = jnp.where(row == column, 1.0, 0.0).astype(F32)
        moving[1] = quarter[...]
        moving[2] = half[...]
        join(half, third, moving.at[3])
        starts = moving
    else:
        starts = given
        factor = base_powers.at[0]
    g = gain[...]
    retain = 1.0 - g

    @pl.loop(0, lanes // 2)
    def _(pair):
        for i in range(2):
            for u in range(2):
                c = 2 * pair + u
                k = 2 * c + i
                t = c * depth + i + (0 if first else 2)
                source = starts if i == 0 else moving
                predicted = dot_nt(source[c], jac[t])
                pi[k] = predicted
                offset = g * obs[pl.ds(t, 1), :]
                if i == 0 or first:
                    dest = moving if i == 0 else phi
                    dest[c, :n] = predicted[:n] * retain
                    dest[c, n:] = predicted[n:] * retain + offset
                change = -(predicted * g)
                dest = pairs if i == 0 else later
                dest[c, :n] = change[:n]
                dest[c, n:] = change[n:] + offset

    if first:
        moving[0, :n] = smooth[...].T

    @pl.loop(0, lanes)
    def _(c):
        pairs[c] = pairs[c] + dot_nn(later[c], factor[...] if not first else moving[0, :n])

    if not first:
        @pl.loop(0, lanes)
        def _(c):
            later[c] = even[c] + dot_nn(pairs[c], base_powers[1])

        halves = [later[c] + dot_nn(later[c + 1], base_powers[2]) for c in (0, 2)]
        offset_map[...] = halves[0] + dot_nn(halves[1], base_powers[3])


def maps(first, starts, jac, obs, gain, factor):
    n = jac.shape[1]
    size = n + PAD
    four = (4, size, n)
    shapes = [(8, size, n)] + ([four, four] if first else [(size, n)])
    scratch = [four, four] + ([] if first else [four])
    return kernel_call(
        functools.partial(maps_body, first),
        shapes,
        [VMEM] * (len(starts) + 4),
        (*starts, jac, obs, gain, factor),
        "maps",
        scratch=[pltpu.VMEM(x, F32) for x in scratch],
        flops=1,
        size=1,
        grant=8,
    )


def base_powers_body(smooth, out):
    out[0] = smooth[...].T

    @pl.loop(1, out.shape[0])
    def _(k):
        out[k] = dot_nn(out[k - 1], out[k - 1])


def high_powers_body(base_powers, out):
    out[0] = base_powers[base_powers.shape[0] - 1]

    @pl.loop(1, out.shape[0])
    def _(k):
        out[k] = dot_nn(out[k - 1], out[k - 1])


def offsets_join_body(level, inner, outer, own_map, other_map, own, other, high, through, out):
    n = out.shape[1]
    is_late = late(inner, outer, level)
    early_map = jnp.where(is_late, other_map[...], own_map[...])
    later = jnp.where(is_late, own[...], other[...])
    moved = dot_nn(early_map, later[:n])
    through[:n] = moved[:n]
    through[n:] = moved[n:] + later[n:]
    out[...] = jnp.where(is_late, other[...], own[...]) + dot_nn(through[...], high[level])


def inside_body(level, inner, outer, other_map, through, high, *refs):
    before_out, behind_out, lift_out = refs[-3:]
    n = high.shape[2]
    is_late = late(inner, outer, level)
    if level == 0:
        row = lax.broadcasted_iota(jnp.int32, (n + PAD, n), 0)
        column = lax.broadcasted_iota(jnp.int32, (n + PAD, n), 1)
        eye = jnp.where(row == column, 1.0, 0.0).astype(F32)
        before_out[...] = jnp.where(is_late, other_map[...], eye)
        behind_out[...] = jnp.where(is_late, jnp.zeros_like(eye), through[...])
        lift_out[...] = jnp.where(is_late, eye[:n], high[level])
        return
    before, behind, lift = refs[:3]
    first = jnp.where(is_late, other_map[...], through[...])
    moved = dot_nn(first, jnp.where(is_late, behind[:n], lift[...]))
    kept = behind[...]
    behind_out[:n] = moved[:n] + jnp.where(is_late, jnp.zeros_like(kept[:n]), kept[:n])
    behind_out[n:] = moved[n:] + kept[n:]
    second = jnp.where(is_late, other_map[:n], lift[...])
    moved = dot_nn(second, jnp.where(is_late, before[:n], high[level]))
    edge = dot_nn(other_map[n:], before[:n]) + before[n:]
    before_out[:n] = jnp.where(is_late, moved, before[:n])
    before_out[n:] = jnp.where(is_late, edge, before[n:])
    lift_out[...] = jnp.where(is_late, lift[...], moved)


def entry_map_body(inner, outer, twin, chip_map, out):
    n = out.shape[1]
    row = lax.broadcasted_iota(jnp.int32, (n + PAD, n), 0)
    column = lax.broadcasted_iota(jnp.int32, (n + PAD, n), 1)
    eye = jnp.where(row == column, 1.0, 0.0).astype(F32)
    out[...] = jnp.where(late(inner, outer, 4), twin[...], eye)

    @pl.when(late(inner, outer, 5))
    def _():
        moved = dot_nn(chip_map[...], out[:n])
        later = out[n:]
        out[:n] = moved[:n]
        out[n:] = moved[n:] + later


def offset_body(outer, first, arrived, near, far, skipped, entry_map, offset_map, entry, offset):
    n = entry_map.shape[1]
    here = jnp.right_shift(outer[0], 2)
    state = dot_nn(far[...], skipped[:n]) + skipped[n:]
    state = jnp.where(here == 3, state, near[...])
    state = jnp.where(here == 1, arrived[...], state)
    state = jnp.where(here == 0, jnp.broadcast_to(first[...], (PAD, n)), state)
    state = dot_nn(state, entry_map[:n]) + entry_map[n:]
    entry[...] = state
    offset[...] = dot_nn(state, offset_map[:n]) + offset_map[n:]


def spread_body(level, inner, outer, own, other, high, out):
    is_late = late(inner, outer, level)
    early_half = jnp.where(is_late, other[...], own[...])
    late_half = jnp.where(is_late, own[...], other[...])
    out[...] = early_half + dot_nn(late_half, high[level])


def ends_body(inner, outer, lift, base_powers, high, *ends):
    ends[0][...] = dot_nn(lift[...], base_powers[0])
    for k in range(len(ends) - 1):
        moved = dot_nn(ends[k][...], high[4 + k])
        ends[k + 1][...] = jnp.where(late(inner, outer, 4 + k), ends[k][...], moved)


def states_body(entry, before, even, odd, obs, gain, pred, filt):
    steps, n = pred.shape
    g = gain[...]
    state = dot_nn(entry[...], before[:n]) + before[n:]

    @pl.loop(0, 4)
    def _(c):
        for i in range(4):
            t = 4 * c + i
            pi = even if i < 2 else odd
            k = 2 * c + i % 2
            predicted = (dot_nn(state, pi[k, :n]) + pi[k, n:])[:1]
            pred[pl.ds(t, 1), :] = predicted
            filt[pl.ds(t, 1), :] = predicted + g * (obs[pl.ds(t, 1), :] - predicted)


def local_body(pred, filt, base_powers, base, shifted):
    steps, n = pred.shape
    local = filt[...] - pred[...]
    shifted[steps:, :] = jnp.zeros((steps, n), F32)
    level = 0
    reach = 1
    while reach < steps:
        shifted[:steps, :] = local
        local = local + dot_nn(shifted[reach : reach + steps, :], base_powers[level])
        reach *= 2
        level += 1
    base[...] = pred[...] + local


def gather_body(inner, outer, entry, behind, base_powers, *refs):
    count = len(refs) // 2
    others, ends, out = refs[:count], refs[count : 2 * count], refs[2 * count]
    n = entry.shape[1]
    inside = dot_nn(entry[...], behind[:n]) + behind[n:]
    value = dot_nn(inside, base_powers[0])
    for k in range(count):
        other = others[k][...]
        other = jnp.where(late(inner, outer, 4 + k), jnp.zeros_like(other), other)
        value = value + dot_nn(other, ends[k][...])
    out[...] = value


def backward_body(inner, outer, other, end, back, base_powers, base, out):
    steps, n = base.shape
    value = other[...]
    value = jnp.where(late(inner, outer, 7), jnp.zeros_like(value), value)
    value = back[...] + dot_nn(value, end[...])
    left = steps - 1 - lax.broadcasted_iota(jnp.int32, (steps, n), 0)
    value = jnp.concatenate([value, value], 0)
    for level in range(base_powers.shape[0] - 1):
        value = jnp.where((left >> level) % 2 == 1, dot_nn(value, base_powers[level]), value)
    out[...] = base[...] + value


def shards(jac, obs, gain_filter, gain_smooth, init_mean):
    steps, n, _ = jac.shape
    inner_count, outer_count = lax.axis_size("inner"), lax.axis_size("outer")
    counts = {"inner": inner_count, "outer": outer_count}
    place = [lax.axis_index(axis).astype(jnp.int32)[None] for axis in ("inner", "outer")]
    gain = gain_filter[None, :]
    first = init_mean[None, :]

    def exchange(total, axis, flip, beside):
        other = lax.ppermute(total, axis, [(i, i ^ flip) for i in range(counts[axis])])
        work = beside()
        return lax.optimization_barrier((other, work))

    with jax.named_scope("compose"):
        total, quarter, half, third, loaded = local_map(place, jac, obs, gain)

    def base_work():
        levels = steps.bit_length()
        return kernel_call(
            base_powers_body,
            (levels, n, n),
            [VMEM],
            (gain_smooth,),
            "base_powers",
            flops=1,
            size=1,
        )

    aside = []

    def offsets_join(level, own_map, other_map, own, other):
        return kernel_call(
            functools.partial(offsets_join_body, level),
            [(n + PAD, n), (n + PAD, n)],
            [SMEM] * 2 + [VMEM] * 5,
            (*place, own_map, other_map, own, other, high),
            "offsets_join",
            flops=1,
            size=1,
            grant=6,
        )

    def inside(level, other_map, through):
        aside[:] = kernel_call(
            functools.partial(inside_body, level),
            [(n + PAD, n), (n + PAD, n), (n, n)],
            [SMEM] * 2 + [VMEM] * (3 + len(aside)),
            (*place, other_map, through, high, *aside),
            "inside",
            flops=1,
            size=1,
        )

    def partner(value, axis, flip):
        return lax.ppermute(value, axis, [(i, i ^ flip) for i in range(counts[axis])])

    own_maps, other_maps = [total], []
    with jax.named_scope("join_0"):
        other, (pi_even, even, phi) = exchange(
            total,
            "inner",
            1,
            lambda: maps(True, (quarter, half, third), loaded, obs, gain, gain_smooth),
        )
        other_maps.append(other)
        own_maps.append(total_call(0, place, own_maps[0], other))
    with jax.named_scope("join_1"):

        def work():
            base_powers = base_work()
            pi_odd, offset_map = maps(False, (phi, even), loaded, obs, gain, base_powers)
            return base_powers, pi_odd, offset_map

        other, (base_powers, pi_odd, offsets) = exchange(own_maps[1], "inner", 3, work)
        other_maps.append(other)
        own_maps.append(total_call(1, place, own_maps[1], other))
    with jax.named_scope("join_2"):

        def work():
            return kernel_call(
                high_powers_body,
                (7, n, n),
                [VMEM],
                (base_powers,),
                "high_powers",
                flops=1,
                size=1,
            )

        far = partner(offsets, "inner", 1)
        other, high = exchange(own_maps[2], "inner", 4, work)
        other_maps.append(other)
        own_maps.append(total_call(2, place, own_maps[2], other))
    with jax.named_scope("join_3"):

        def work():
            through, joined = offsets_join(0, own_maps[0], other_maps[0], offsets, far)
            return through, joined, partner(joined, "inner", 3)

        other = partner(own_maps[3], "inner", 12)
        through, offsets, far = work()
        other, through = lax.optimization_barrier((other, through))
        other_maps.append(other)
        own_maps.append(total_call(3, place, own_maps[3], other))
    with jax.named_scope("join_core"):
        twin = partner(own_maps[4], "outer", 1)
        own_maps.append(total_call(4, place, own_maps[4], twin))
    with jax.named_scope("join_z"):
        chip_map = partner(own_maps[5], "outer", 2)
        inside(0, other_maps[0], through)
        far, _ = lax.optimization_barrier((far, own_maps[5]))
        through, offsets = offsets_join(1, own_maps[1], other_maps[1], offsets, far)
        far = partner(offsets, "inner", 4)
        inside(1, other_maps[1], through)
        chip_map, aside[:] = lax.optimization_barrier((chip_map, aside))
        total = total_call(5, place, own_maps[5], chip_map)

    group = outer_count // 4
    def mirror(source, dest):
        return [
            (source * group + z * 2 + c, dest * group + (group // 2 - 1 - z) * 2 + c)
            for z in range(group // 2)
            for c in range(2)
        ]

    with jax.named_scope("hop_0"):
        y = hop(0, place, first, first, total)
        arrived = lax.ppermute(y, "outer", mirror(0, 1))
        far, _ = lax.optimization_barrier((far, y))
        through, offsets = offsets_join(2, own_maps[2], other_maps[2], offsets, far)
        far = partner(offsets, "inner", 12)
        arrived, through = lax.optimization_barrier((arrived, through))
    with jax.named_scope("hop_1"):
        y = hop(1, place, first, arrived, total)
        near = lax.ppermute(y, "outer", mirror(1, 2))
        farther = lax.ppermute(y, "outer", mirror(1, 3))
        sent_map, _ = lax.optimization_barrier((total, y))
        skipped = lax.ppermute(sent_map, "outer", mirror(2, 3))
        entry_map = kernel_call(
            entry_map_body,
            (n + PAD, n),
            [SMEM] * 2 + [VMEM] * 2,
            (*place, twin, chip_map),
            "entry_map",
            flops=1,
            size=1,
        )
        inside(2, other_maps[2], through)
        far, _ = lax.optimization_barrier((far, y))
        through, offsets = offsets_join(3, own_maps[3], other_maps[3], offsets, far)
        near, farther, offsets, entry_map, aside[:] = lax.optimization_barrier(
            (near, farther, offsets, entry_map, aside)
        )
    with jax.named_scope("offset"):
        entry, value = kernel_call(
            offset_body,
            [(PAD, n), (PAD, n)],
            [SMEM] + [VMEM] * 7,
            (place[1], first, arrived, near, farther, skipped, entry_map, offsets),
            "offset",
            flops=300 * n * n,
            size=12 * n * n,
        )

    def spread(level, value, other):
        return kernel_call(
            functools.partial(spread_body, level),
            (PAD, n),
            [SMEM] * 2 + [VMEM] * 3,
            (*place, value, other, high),
            "spread",
            flops=96 * n * n,
            size=4 * n * n,
        )

    others = []
    with jax.named_scope("spread_core"):
        others.append(partner(value, "outer", 1))
        value = spread(4, value, others[0])
    with jax.named_scope("spread_z0"):
        other = partner(value, "outer", 2)
        inside(3, other_maps[3], through)
        ends = kernel_call(
            ends_body,
            [(n, n)] * 4,
            [SMEM] * 2 + [VMEM] * 3,
            (*place, aside[2], base_powers, high),
            "ends",
            flops=1,
            size=1,
        )
        other, ends, aside[:] = lax.optimization_barrier((other, ends, aside))
        others.append(other)
        value = spread(5, value, other)
    with jax.named_scope("spread_z1"):
        other = partner(value, "outer", 4)
        pred, filt = kernel_call(
            states_body,
            [(steps, n), (steps, n)],
            [VMEM] * 6,
            (entry, aside[0], pi_even, pi_odd, obs, gain),
            "states",
            flops=1,
            size=1,
        )
        other, pred = lax.optimization_barrier((other, pred))
        others.append(other)
        value = spread(6, value, other)
    with jax.named_scope("spread_z2"):
        other = partner(value, "outer", 14)
        base = kernel_call(
            local_body,
            (steps, n),
            [VMEM] * 3,
            (pred, filt, base_powers),
            "local",
            scratch=[pltpu.VMEM((2 * steps, n), F32)],
            flops=1,
            size=1,
        )
        back = kernel_call(
            gather_body,
            (PAD, n),
            [SMEM] * 2 + [VMEM] * 9,
            (*place, entry, aside[1], base_powers, *others, *ends[:3]),
            "gather",
            flops=1,
            size=1,
        )
        other, base, back = lax.optimization_barrier((other, base, back))
    with jax.named_scope("backward"):
        smoothed = kernel_call(
            backward_body,
            (steps, n),
            [SMEM] * 2 + [VMEM] * 5,
            (*place, other, ends[3], back, base_powers, base),
            "backward",
            flops=600 * n * n,
            size=24 * n * n,
        )
    return (filt, smoothed)


def solution(mesh):
    return jax.shard_map(
        shards,
        mesh=mesh,
        in_specs=(P(("outer", "inner"), None, None), P(("outer", "inner"), None), P(), P(), P()),
        out_specs=(P(("outer", "inner"), None), P(("outer", "inner"), None)),
        check_vma=False,
    )
```

profile of v0, /device:TPU:1, one launch (start us, length us, event | category | flops | bytes accessed | tf_op | source)
XLA Modules:
  0.0 107.5 jit_solution(4014821843119921723)
XLA Ops:
  2.0 9.2 %local_map.1 = (f32[264,256]{1,0:T(8,128)S(1)}, f32[264,256]{1,0:T(8,128)S(1)}, f32[264,256]{1,0:T(8,128)S(1)}, f32[264,256]{1,0:T(8,128)S(1)}, f32[16,256,256]{2,1,0:T(8,128)S(1)}) custom-call(s32[1]{0:T(128)} %bitcast.2.inner, s32[1]{0:T(128)} %bitcast.outer, f32[16,256,256]{2,1,0:T(8,128)} %jac_hbm.1, f32[16,256]{1,0:T(8,128)S(1)} %copy-done.1, ...), custom_call_target="tpu_custom_call" | custom-call | flops 3221225472 | bytes 4194304 | tf_op jit(solution)/shard_map/compose/local_map/pallas_call | solution.py:33
  11.3 2.2 %collective-permute-start = (f32[264,256]{1,0:T(8,128)S(1)}, f32[264,256]{1,0:T(8,128)S(1)}, u32[]{:S(2)}, u32[]{:S(2)}) collective-permute-start(f32[264,256]{1,0:T(8,128)S(1)} %get-tuple-element.81.own.own_map), channel_id=1, source_target_pairs={{0,16},{16,0},{32,48},{48,32},{64,80},{80,64},{96,112},{112,96},{1... | collective-permute-start | bytes 811016 | tf_op jit(solution)/shard_map/join_0/ppermute | solution.py:401
  13.5 4.8 %maps.2 = (f32[8,264,256]{2,1,0:T(8,128)S(1)}, f32[4,264,256]{2,1,0:T(8,128)S(1)}, f32[4,264,256]{2,1,0:T(8,128)S(1)}) custom-call(f32[264,256]{1,0:T(8,128)S(1)} %get-tuple-element.82.refs_0_, f32[264,256]{1,0:T(8,128)S(1)} %get-tuple-element.83.refs_1_, f32[264,256]{1,0:T(8,128)S(1)} %get-tuple-element.84.refs_2_, ...), custom_call_target="tpu_custom_call" | custom-call | flops 1 | bytes 1 | tf_op jit(solution)/shard_map/join_0/maps/pallas_call | solution.py:33
  18.9 4.1 %collective-permute-start.1 = (f32[264,256]{1,0:T(8,128)S(1)}, f32[264,256]{1,0:T(8,128)S(1)}, u32[]{:S(2)}, u32[]{:S(2)}) collective-permute-start(f32[264,256]{1,0:T(8,128)S(1)} %total.6.own.own_map), channel_id=1, source_target_pairs={{0,48},{16,32},{32,16},{48,0},{64,112},{80,96},{96,80},{112,64},{1... | collective-permute-start | bytes 811016 | tf_op jit(solution)/shard_map/join_1/ppermute | solution.py:401
  22.9 1.7 %base_powers.1.refs_5_ = f32[5,256,256]{2,1,0:T(8,128)S(1)} custom-call(f32[256,256]{1,0:T(8,128)S(1)} %copy-done), custom_call_target="tpu_custom_call" | custom-call | flops 1 | bytes 1 | tf_op jit(solution)/shard_map/join_1/base_powers/pallas_call | solution.py:33
  24.7 7.0 %maps.3 = (f32[8,264,256]{2,1,0:T(8,128)S(1)}, f32[264,256]{1,0:T(8,128)S(1)}) custom-call(f32[4,264,256]{2,1,0:T(8,128)S(1)} %get-tuple-element.90.refs_0_, f32[4,264,256]{2,1,0:T(8,128)S(1)} %get-tuple-element.91.refs_1_, f32[16,256,256]{2,1,0:T(8,128)S(1)} %get-tuple-element.85.refs_3_.refs_2_, f32[16,256]{1,0:T(8,128)S(1)} %copy-done.1, ...), custom_call_target="tpu_custom_call" | custom-call | flops 1 | bytes 1 | tf_op jit(solution)/shard_map/join_1/maps/pallas_call | solution.py:33
  32.1 1.3 %collective-permute-start.2 = (f32[264,256]{1,0:T(8,128)S(1)}, f32[264,256]{1,0:T(8,128)S(1)}, u32[]{:S(2)}, u32[]{:S(2)}) collective-permute-start(f32[264,256]{1,0:T(8,128)S(1)} %total.7.own.own_map), channel_id=1, source_target_pairs={{0,64},{16,80},{32,96},{48,112},{64,0},{80,16},{96,32},{112,48},{1... | collective-permute-start | bytes 811016 | tf_op jit(solution)/shard_map/join_2/ppermute | solution.py:401
  33.3 2.4 %high_powers.1.high = f32[7,256,256]{2,1,0:T(8,128)S(1)} custom-call(f32[5,256,256]{2,1,0:T(8,128)S(1)} %base_powers.1.refs_5_), custom_call_target="tpu_custom_call" | custom-call | flops 1 | bytes 1 | tf_op jit(solution)/shard_map/join_2/high_powers/pallas_call | solution.py:33
  35.7 2.6 %collective-permute-done.2.other.other_map = f32[264,256]{1,0:T(8,128)S(1)} collective-permute-done((f32[264,256]{1,0:T(8,128)S(1)}, f32[264,256]{1,0:T(8,128)S(1)}, u32[]{:S(2)}, u32[]{:S(2)}) %collective-permute-start.2) | collective-permute-done | bytes 270368 | tf_op jit(solution)/shard_map/join_2/ppermute | solution.py:401
  38.7 2.5 %collective-permute-start.3 = (f32[264,256]{1,0:T(8,128)S(1)}, f32[264,256]{1,0:T(8,128)S(1)}, u32[]{:S(2)}, u32[]{:S(2)}) collective-permute-start(f32[264,256]{1,0:T(8,128)S(1)} %total.8.own.own_map), channel_id=1, source_target_pairs={{0,192},{16,208},{32,224},{48,240},{64,128},{80,144},{96,160},{112... | collective-permute-start | bytes 811016 | tf_op jit(solution)/shard_map/join_3/ppermute | solution.py:446
  42.3 3.0 %collective-permute-done.3.other.other_map = f32[264,256]{1,0:T(8,128)S(1)} collective-permute-done((f32[264,256]{1,0:T(8,128)S(1)}, f32[264,256]{1,0:T(8,128)S(1)}, u32[]{:S(2)}, u32[]{:S(2)}) %collective-permute-start.3) | collective-permute-done | bytes 270368 | tf_op jit(solution)/shard_map/join_3/ppermute | solution.py:446
  45.7 4.0 %collective-permute-start.5 = (f32[264,256]{1,0:T(8,128)S(1)}, f32[264,256]{1,0:T(8,128)S(1)}, u32[]{:S(2)}, u32[]{:S(2)}) collective-permute-start(f32[264,256]{1,0:T(8,128)S(1)} %total.9.own), channel_id=1, source_target_pairs={{0,1},{1,0},{2,3},{3,2},{4,5},{5,4},{6,7},{7,6},{8,9},{9,8},{10,11... | collective-permute-start | bytes 811016 | tf_op jit(solution)/shard_map/join_core/ppermute | solution.py:446
  51.3 1.7 %collective-permute-start.6 = (f32[264,256]{1,0:T(8,128)S(1)}, f32[264,256]{1,0:T(8,128)S(1)}, u32[]{:S(2)}, u32[]{:S(2)}) collective-permute-start(f32[264,256]{1,0:T(8,128)S(1)} %total.10.own), channel_id=1, source_target_pairs={{0,2},{1,3},{2,0},{3,1},{4,6},{5,7},{6,4},{7,5},{8,10},{9,11},{10,... | collective-permute-start | bytes 811016 | tf_op jit(solution)/shard_map/join_z/ppermute | solution.py:446
  53.0 5.9 %collective-permute-done.7.other = f32[264,256]{1,0:T(8,128)S(1)} collective-permute-done((f32[264,256]{1,0:T(8,128)S(1)}, f32[264,256]{1,0:T(8,128)S(1)}, u32[]{:S(2)}, u32[]{:S(2)}) %collective-permute-start.7) | collective-permute-done | bytes 270368 | tf_op jit(solution)/shard_map/join_3/ppermute | solution.py:446
  61.7 6.5 %collective-permute-start.8 = (f32[8,256]{1,0:T(8,128)S(1)}, f32[8,256]{1,0:T(8,128)S(1)}, u32[]{:S(2)}, u32[]{:S(2)}) collective-permute-start(f32[8,256]{1,0:T(8,128)S(1)} %hop.2), channel_id=1, source_target_pairs={{0,6},{1,7},{2,4},{3,5},{16,22},{17,23},{18,20},{19,21},{32,38},{3... | collective-permute-start | bytes 24584 | tf_op jit(solution)/shard_map/hop_0/ppermute | solution.py:519
  69.2 2.6 %collective-permute-start.12 = (f32[264,256]{1,0:T(8,128)S(1)}, f32[264,256]{1,0:T(8,128)S(1)}, u32[]{:S(2)}, u32[]{:S(2)}) collective-permute-start(f32[264,256]{1,0:T(8,128)S(1)} %get-tuple-element.116.own), channel_id=1, source_target_pairs={{0,192},{16,208},{32,224},{48,240},{64,128},{80,144},{96,160},{112... | collective-permute-start | bytes 811016 | tf_op jit(solution)/shard_map/hop_0/ppermute | solution.py:446
  74.9 2.2 %collective-permute-done.12.other = f32[264,256]{1,0:T(8,128)S(1)} collective-permute-done((f32[264,256]{1,0:T(8,128)S(1)}, f32[264,256]{1,0:T(8,128)S(1)}, u32[]{:S(2)}, u32[]{:S(2)}) %collective-permute-start.12) | collective-permute-done | bytes 270368 | tf_op jit(solution)/shard_map/hop_0/ppermute | solution.py:446
  79.0 2.4 %collective-permute-start.14 = (f32[8,256]{1,0:T(8,128)S(1)}, f32[8,256]{1,0:T(8,128)S(1)}, u32[]{:S(2)}, u32[]{:S(2)}) collective-permute-start(f32[8,256]{1,0:T(8,128)S(1)} %get-tuple-element.132.own), channel_id=1, source_target_pairs={{0,1},{1,0},{2,3},{3,2},{4,5},{5,4},{6,7},{7,6},{8,9},{9,8},{10,11... | collective-permute-start | bytes 24584 | tf_op jit(solution)/shard_map/spread_core/ppermute | solution.py:446
  83.9 1.9 %ends.1 = (f32[256,256]{1,0:T(8,128)S(1)}, f32[256,256]{1,0:T(8,128)S(1)}, f32[256,256]{1,0:T(8,128)S(1)}, f32[256,256]{1,0:T(8,128)S(1)}) custom-call(s32[1]{0:T(128)} %bitcast.2.inner, s32[1]{0:T(128)} %bitcast.outer, f32[256,256]{1,0:T(8,128)S(1)} %get-tuple-element.137.lift, f32[5,256,256]{2,1,0:T(8,128)S(1)} %base_powers.1.refs_5_, ...), custom_call_target="tpu_custom_call" | custom-call | flops 1 | bytes 1 | tf_op jit(solution)/shard_map/spread_z0/ends/pallas_call | solution.py:33
  86.0 8.4 %collective-permute-start.16 = (f32[8,256]{1,0:T(8,128)S(1)}, f32[8,256]{1,0:T(8,128)S(1)}, u32[]{:S(2)}, u32[]{:S(2)}) collective-permute-start(f32[8,256]{1,0:T(8,128)S(1)} %spread.4.own), channel_id=1, source_target_pairs={{0,4},{1,5},{2,6},{3,7},{4,0},{5,1},{6,2},{7,3},{8,12},{9,13},{10,... | collective-permute-start | bytes 24584 | tf_op jit(solution)/shard_map/spread_z1/ppermute | solution.py:446
  94.5 3.2 %states.1 = (f32[16,256]{1,0:T(8,128)S(1)}, f32[16,256]{1,0:T(8,128)}) custom-call(f32[8,256]{1,0:T(8,128)S(1)} %get-tuple-element.131.entry, f32[264,256]{1,0:T(8,128)S(1)} %get-tuple-element.144.before, f32[8,264,256]{2,1,0:T(8,128)S(1)} %get-tuple-element.145.even, f32[8,264,256]{2,1,0:T(8,128)S(1)} %get-tuple-element.146.odd, f32[16,256]{1,0:T(8,128)S(1)} %copy-done.1, ...), custom_call_target="tpu_custom_call" | custom-call | flops 1 | bytes 1 | tf_op jit(solution)/shard_map/spread_z1/states/pallas_call | solution.py:33
  97.9 4.7 %collective-permute-start.17 = (f32[8,256]{1,0:T(8,128)S(1)}, f32[8,256]{1,0:T(8,128)S(1)}, u32[]{:S(2)}, u32[]{:S(2)}) collective-permute-start(f32[8,256]{1,0:T(8,128)S(1)} %spread.5), channel_id=1, source_target_pairs={{0,14},{1,15},{2,12},{3,13},{4,10},{5,11},{6,8},{7,9},{8,6},{9,7},... | collective-permute-start | bytes 24584 | tf_op jit(solution)/shard_map/spread_z2/ppermute | solution.py:446
  103.3 1.2 %local.1.base = f32[16,256]{1,0:T(8,128)S(1)} custom-call(f32[16,256]{1,0:T(8,128)S(1)} %get-tuple-element.151.pred, f32[16,256]{1,0:T(8,128)S(1)} %copy-done.2, f32[5,256,256]{2,1,0:T(8,128)S(1)} %base_powers.1.refs_5_), custom_call_target="tpu_custom_call" | custom-call | flops 1 | bytes 1 | tf_op jit(solution)/shard_map/spread_z2/local/pallas_call | solution.py:33
  105.4 2.0 %backward.1 = f32[16,256]{1,0:T(8,128)} custom-call(s32[1]{0:T(128)} %bitcast.2.inner, s32[1]{0:T(128)} %bitcast.outer, f32[8,256]{1,0:T(8,128)S(1)} %collective-permute-done.17.other, f32[256,256]{1,0:T(8,128)S(1)} %get-tuple-element.157.end, f32[8,256]{1,0:T(8,128)S(1)} %gather.1.back, f32[5,256,256]{2,1,0:T(8,128)S(1)} %base_powers.1.refs_5_, ...), custom_call_target="tpu_custom_call" | custom-call | flops 39321600 | bytes 1572864 | tf_op jit(solution)/shard_map/backward/backward/pallas_call | solution.py:33
  (53 shorter events, 19.1 us)
Async XLA Ops:
  0.6 0.7 copy-start.1
  1.4 0.7 copy-start.4
  2.0 11.4 %copy-start = (f32[256,256]{1,0:T(8,128)S(1)}, f32[256,256]{1,0:T(8,128)}, u32[]{:S(2)}) copy-start(f32[256,256]{1,0:T(8,128)} %smooth.1) | copy-start | bytes 786436
  11.3 7.2 %collective-permute-start = (f32[264,256]{1,0:T(8,128)S(1)}, f32[264,256]{1,0:T(8,128)S(1)}, u32[]{:S(2)}, u32[]{:S(2)}) collective-permute-start(f32[264,256]{1,0:T(8,128)S(1)} %get-tuple-element.81.own.own_map), channel_id=1, source_target_pairs={{0,16},{16,0},{32,48},{48,32},{64,80},{80,64},{96,112},{112,96},{1... | collective-permute-start | bytes 811016 | tf_op jit(solution)/shard_map/join_0/ppermute | solution.py:401
  18.9 12.8 %collective-permute-start.1 = (f32[264,256]{1,0:T(8,128)S(1)}, f32[264,256]{1,0:T(8,128)S(1)}, u32[]{:S(2)}, u32[]{:S(2)}) collective-permute-start(f32[264,256]{1,0:T(8,128)S(1)} %total.6.own.own_map), channel_id=1, source_target_pairs={{0,48},{16,32},{32,16},{48,0},{64,112},{80,96},{96,80},{112,64},{1... | collective-permute-start | bytes 811016 | tf_op jit(solution)/shard_map/join_1/ppermute | solution.py:401
  32.1 6.2 %collective-permute-start.2 = (f32[264,256]{1,0:T(8,128)S(1)}, f32[264,256]{1,0:T(8,128)S(1)}, u32[]{:S(2)}, u32[]{:S(2)}) collective-permute-start(f32[264,256]{1,0:T(8,128)S(1)} %total.7.own.own_map), channel_id=1, source_target_pairs={{0,64},{16,80},{32,96},{48,112},{64,0},{80,16},{96,32},{112,48},{1... | collective-permute-start | bytes 811016 | tf_op jit(solution)/shard_map/join_2/ppermute | solution.py:401
  33.3 7.9 %collective-permute-start.4 = (f32[264,256]{1,0:T(8,128)S(1)}, f32[264,256]{1,0:T(8,128)S(1)}, u32[]{:S(2)}, u32[]{:S(2)}) collective-permute-start(f32[264,256]{1,0:T(8,128)S(1)} %get-tuple-element.97.own), channel_id=1, source_target_pairs={{0,16},{16,0},{32,48},{48,32},{64,80},{80,64},{96,112},{112,96},{1... | collective-permute-start | bytes 811016 | tf_op jit(solution)/shard_map/join_2/ppermute | solution.py:446
  38.7 6.6 %collective-permute-start.3 = (f32[264,256]{1,0:T(8,128)S(1)}, f32[264,256]{1,0:T(8,128)S(1)}, u32[]{:S(2)}, u32[]{:S(2)}) collective-permute-start(f32[264,256]{1,0:T(8,128)S(1)} %total.8.own.own_map), channel_id=1, source_target_pairs={{0,192},{16,208},{32,224},{48,240},{64,128},{80,144},{96,160},{112... | collective-permute-start | bytes 811016 | tf_op jit(solution)/shard_map/join_3/ppermute | solution.py:446
  45.7 5.2 %collective-permute-start.5 = (f32[264,256]{1,0:T(8,128)S(1)}, f32[264,256]{1,0:T(8,128)S(1)}, u32[]{:S(2)}, u32[]{:S(2)}) collective-permute-start(f32[264,256]{1,0:T(8,128)S(1)} %total.9.own), channel_id=1, source_target_pairs={{0,1},{1,0},{2,3},{3,2},{4,5},{5,4},{6,7},{7,6},{8,9},{9,8},{10,11... | collective-permute-start | bytes 811016 | tf_op jit(solution)/shard_map/join_core/ppermute | solution.py:446
  49.7 9.3 %collective-permute-start.7 = (f32[264,256]{1,0:T(8,128)S(1)}, f32[264,256]{1,0:T(8,128)S(1)}, u32[]{:S(2)}, u32[]{:S(2)}) collective-permute-start(f32[264,256]{1,0:T(8,128)S(1)} %get-tuple-element.101.own), channel_id=1, source_target_pairs={{0,48},{16,32},{32,16},{48,0},{64,112},{80,96},{96,80},{112,64},{1... | collective-permute-start | bytes 811016 | tf_op jit(solution)/shard_map/join_3/ppermute | solution.py:446
  51.3 9.7 %collective-permute-start.6 = (f32[264,256]{1,0:T(8,128)S(1)}, f32[264,256]{1,0:T(8,128)S(1)}, u32[]{:S(2)}, u32[]{:S(2)}) collective-permute-start(f32[264,256]{1,0:T(8,128)S(1)} %total.10.own), channel_id=1, source_target_pairs={{0,2},{1,3},{2,0},{3,1},{4,6},{5,7},{6,4},{7,5},{8,10},{9,11},{10,... | collective-permute-start | bytes 811016 | tf_op jit(solution)/shard_map/join_z/ppermute | solution.py:446
  60.0 8.1 %collective-permute-start.9 = (f32[264,256]{1,0:T(8,128)S(1)}, f32[264,256]{1,0:T(8,128)S(1)}, u32[]{:S(2)}, u32[]{:S(2)}) collective-permute-start(f32[264,256]{1,0:T(8,128)S(1)} %get-tuple-element.112.own), channel_id=1, source_target_pairs={{0,64},{16,80},{32,96},{48,112},{64,0},{80,16},{96,32},{112,48},{1... | collective-permute-start | bytes 811016 | tf_op jit(solution)/shard_map/join_z/ppermute | solution.py:446
  60.2 1.2 %copy-start.3 = (f32[256]{0:T(256)S(1)}, f32[256]{0:T(256)}, u32[]{:S(2)}) copy-start(f32[256]{0:T(256)} %param.9) | copy-start | bytes 3076
  61.7 10.1 %collective-permute-start.8 = (f32[8,256]{1,0:T(8,128)S(1)}, f32[8,256]{1,0:T(8,128)S(1)}, u32[]{:S(2)}, u32[]{:S(2)}) collective-permute-start(f32[8,256]{1,0:T(8,128)S(1)} %hop.2), channel_id=1, source_target_pairs={{0,6},{1,7},{2,4},{3,5},{16,22},{17,23},{18,20},{19,21},{32,38},{3... | collective-permute-start | bytes 24584 | tf_op jit(solution)/shard_map/hop_0/ppermute | solution.py:519
  69.2 7.9 %collective-permute-start.12 = (f32[264,256]{1,0:T(8,128)S(1)}, f32[264,256]{1,0:T(8,128)S(1)}, u32[]{:S(2)}, u32[]{:S(2)}) collective-permute-start(f32[264,256]{1,0:T(8,128)S(1)} %get-tuple-element.116.own), channel_id=1, source_target_pairs={{0,192},{16,208},{32,224},{48,240},{64,128},{80,144},{96,160},{112... | collective-permute-start | bytes 811016 | tf_op jit(solution)/shard_map/hop_0/ppermute | solution.py:446
  72.0 6.2 %collective-permute-start.13 = (f32[264,256]{1,0:T(8,128)S(1)}, f32[264,256]{1,0:T(8,128)S(1)}, u32[]{:S(2)}, u32[]{:S(2)}) collective-permute-start(f32[264,256]{1,0:T(8,128)S(1)} %total.11.group_map), channel_id=1, source_target_pairs={{8,14},{9,15},{10,12},{11,13},{24,30},{25,31},{26,28},{27,29},{40,... | collective-permute-start | bytes 811016 | tf_op jit(solution)/shard_map/hop_1/ppermute | solution.py:529
  72.7 5.5 %collective-permute-start.11 = (f32[8,256]{1,0:T(8,128)S(1)}, f32[8,256]{1,0:T(8,128)S(1)}, u32[]{:S(2)}, u32[]{:S(2)}) collective-permute-start(f32[8,256]{1,0:T(8,128)S(1)} %hop.3), channel_id=1, source_target_pairs={{4,14},{5,15},{6,12},{7,13},{20,30},{21,31},{22,28},{23,29},{36,46... | collective-permute-start | bytes 24584 | tf_op jit(solution)/shard_map/hop_1/ppermute | solution.py:527
  73.4 4.8 %collective-permute-start.10 = (f32[8,256]{1,0:T(8,128)S(1)}, f32[8,256]{1,0:T(8,128)S(1)}, u32[]{:S(2)}, u32[]{:S(2)}) collective-permute-start(f32[8,256]{1,0:T(8,128)S(1)} %hop.3), channel_id=1, source_target_pairs={{4,10},{5,11},{6,8},{7,9},{20,26},{21,27},{22,24},{23,25},{36,42},... | collective-permute-start | bytes 24584 | tf_op jit(solution)/shard_map/hop_1/ppermute | solution.py:526
  79.0 3.2 %collective-permute-start.14 = (f32[8,256]{1,0:T(8,128)S(1)}, f32[8,256]{1,0:T(8,128)S(1)}, u32[]{:S(2)}, u32[]{:S(2)}) collective-permute-start(f32[8,256]{1,0:T(8,128)S(1)} %get-tuple-element.132.own), channel_id=1, source_target_pairs={{0,1},{1,0},{2,3},{3,2},{4,5},{5,4},{6,7},{7,6},{8,9},{9,8},{10,11... | collective-permute-start | bytes 24584 | tf_op jit(solution)/shard_map/spread_core/ppermute | solution.py:446
  82.4 3.4 %collective-permute-start.15 = (f32[8,256]{1,0:T(8,128)S(1)}, f32[8,256]{1,0:T(8,128)S(1)}, u32[]{:S(2)}, u32[]{:S(2)}) collective-permute-start(f32[8,256]{1,0:T(8,128)S(1)} %spread.3.own), channel_id=1, source_target_pairs={{0,2},{1,3},{2,0},{3,1},{4,6},{5,7},{6,4},{7,5},{8,10},{9,11},{10,... | collective-permute-start | bytes 24584 | tf_op jit(solution)/shard_map/spread_z0/ppermute | solution.py:446
  86.0 11.6 %collective-permute-start.16 = (f32[8,256]{1,0:T(8,128)S(1)}, f32[8,256]{1,0:T(8,128)S(1)}, u32[]{:S(2)}, u32[]{:S(2)}) collective-permute-start(f32[8,256]{1,0:T(8,128)S(1)} %spread.4.own), channel_id=1, source_target_pairs={{0,4},{1,5},{2,6},{3,7},{4,0},{5,1},{6,2},{7,3},{8,12},{9,13},{10,... | collective-permute-start | bytes 24584 | tf_op jit(solution)/shard_map/spread_z1/ppermute | solution.py:446
  97.9 7.5 %collective-permute-start.17 = (f32[8,256]{1,0:T(8,128)S(1)}, f32[8,256]{1,0:T(8,128)S(1)}, u32[]{:S(2)}, u32[]{:S(2)}) collective-permute-start(f32[8,256]{1,0:T(8,128)S(1)} %spread.5), channel_id=1, source_target_pairs={{0,14},{1,15},{2,12},{3,13},{4,10},{5,11},{6,8},{7,9},{8,6},{9,7},... | collective-permute-start | bytes 24584 | tf_op jit(solution)/shard_map/spread_z2/ppermute | solution.py:446
  102.6 0.7 copy-start.2
where the time goes:
time: 108 us; the launch traced here: 107 us
  Pallas kernels  45.4 us (42%)
  starting transfers between devices  43.1 us (40%)
  waiting for transfers between devices  15.9 us (15%)
  local copies, waits for them, and re-layouts  2.12 us (2%)
    pallas_call x31, Pallas kernels, kernel_call(): pl.pallas_call(body, out_shape=shapes, in_specs=in_specs, out_specs=out_s...  45.4 us
    ppermute x11, starting transfers between devices, partner(): lax.ppermute(value, axis, [(i, i ^ flip) for i in range(counts[axis])])  27.1 us
    ppermute x11, waiting for transfers between devices, partner(): lax.ppermute(value, axis, [(i, i ^ flip) for i in range(counts[axis])])  13.1 us
    ppermute x3, starting transfers between devices, exchange(): lax.ppermute(total, axis, [(i, i ^ flip) for i in range(counts[axis])])  7.59 us
    ppermute x1, starting transfers between devices, shards(): arrived = lax.ppermute(y, 'outer', mirror(0, 1))  6.45 us
    ppermute x3, waiting for transfers between devices, exchange(): lax.ppermute(total, axis, [(i, i ^ flip) for i in range(counts[axis])])  2.74 us
  transfers between devices with their start and end apart: 18, of which 7 were waited for; matrix products, arithmetic and copies ran while one was open for 0% of the time, Pallas kernels for 29%

commit v1 on v0

--- a/solution.py
+++ b/solution.py
@@ -165,8 +165,8 @@
         quarter, half, third, jac, obs, gain, smooth, pi, pairs, phi = refs[:10]
         later, moving = refs[10:]
     else:
-        given, even, jac, obs, gain, base_powers, pi, offset_map = refs[:8]
-        later, moving, pairs = refs[8:]
+        given, jac, obs, gain, base_powers, pi, pairs = refs[:7]
+        later, moving = refs[7:]
     n = jac.shape[1]
     size = n + PAD
     lanes = 4
@@ -185,8 +185,7 @@
     g = gain[...]
     retain = 1.0 - g
 
-    @pl.loop(0, lanes // 2)
-    def _(pair):
+    def two(pair):
         for i in range(2):
             for u in range(2):
                 c = 2 * pair + u
@@ -206,27 +205,33 @@
                 dest[c, n:] = change[n:] + offset
 
     if first:
+        pl.loop(0, lanes // 2)(two)
+    else:
+        two(0)
+        two(1)
+    if first:
         moving[0, :n] = smooth[...].T
 
     @pl.loop(0, lanes)
     def _(c):
         pairs[c] = pairs[c] + dot_nn(later[c], factor[...] if not first else moving[0, :n])
 
-    if not first:
-        @pl.loop(0, lanes)
-        def _(c):
-            later[c] = even[c] + dot_nn(pairs[c], base_powers[1])
-
-        halves = [later[c] + dot_nn(later[c + 1], base_powers[2]) for c in (0, 2)]
-        offset_map[...] = halves[0] + dot_nn(halves[1], base_powers[3])
+
+def offset_map_body(even, odd, base_powers, out, quads):
+    @pl.loop(0, quads.shape[0])
+    def _(c):
+        quads[c] = even[c] + dot_nn(odd[c], base_powers[1])
+
+    halves = [quads[c] + dot_nn(quads[c + 1], base_powers[2]) for c in (0, 2)]
+    out[...] = halves[0] + dot_nn(halves[1], base_powers[3])
 
 
 def maps(first, starts, jac, obs, gain, factor):
     n = jac.shape[1]
     size = n + PAD
     four = (4, size, n)
-    shapes = [(8, size, n)] + ([four, four] if first else [(size, n)])
-    scratch = [four, four] + ([] if first else [four])
+    shapes = [(8, size, n), four] + ([four] if first else [])
+    scratch = [four, four]
     return kernel_call(
         functools.partial(maps_body, first),
         shapes,
@@ -234,8 +239,8 @@
         (*starts, jac, obs, gain, factor),
         "maps",
         scratch=[pltpu.VMEM(x, F32) for x in scratch],
-        flops=1,
-        size=1,
+        flops=12 * 8 * n**3,
+        size=8 * 12 * n * n,
         grant=8,
     )
 
@@ -293,19 +298,18 @@
     lift_out[...] = jnp.where(is_late, lift[...], moved)
 
 
-def entry_map_body(inner, outer, twin, chip_map, out):
+def entry_map_body(inner, outer, row_map, twin, chip_map, out):
     n = out.shape[1]
     row = lax.broadcasted_iota(jnp.int32, (n + PAD, n), 0)
     column = lax.broadcasted_iota(jnp.int32, (n + PAD, n), 1)
     eye = jnp.where(row == column, 1.0, 0.0).astype(F32)
-    out[...] = jnp.where(late(inner, outer, 4), twin[...], eye)
-
-    @pl.when(late(inner, outer, 5))
-    def _():
-        moved = dot_nn(chip_map[...], out[:n])
-        later = out[n:]
-        out[:n] = moved[:n]
-        out[n:] = moved[n:] + later
+    out[...] = jnp.where(late(inner, outer, 3), row_map[...], eye)
+    for level, earlier in ((4, twin), (5, chip_map)):
+        is_late = late(inner, outer, level)
+        moved = dot_nn(earlier[...], out[:n])
+        later = out[...]
+        out[:n] = jnp.where(is_late, moved[:n], later[:n])
+        out[n:] = jnp.where(is_late, moved[n:] + later[n:], later[n:])
 
 
 def offset_body(outer, first, arrived, near, far, skipped, entry_map, offset_map, entry, offset):
@@ -330,8 +334,8 @@
 def ends_body(inner, outer, lift, base_powers, high, *ends):
     ends[0][...] = dot_nn(lift[...], base_powers[0])
     for k in range(len(ends) - 1):
-        moved = dot_nn(ends[k][...], high[4 + k])
-        ends[k + 1][...] = jnp.where(late(inner, outer, 4 + k), ends[k][...], moved)
+        moved = dot_nn(ends[k][...], high[3 + k])
+        ends[k + 1][...] = jnp.where(late(inner, outer, 3 + k), ends[k][...], moved)
 
 
 def states_body(entry, before, even, odd, obs, gain, pred, filt):
@@ -372,7 +376,7 @@
     value = dot_nn(inside, base_powers[0])
     for k in range(count):
         other = others[k][...]
-        other = jnp.where(late(inner, outer, 4 + k), jnp.zeros_like(other), other)
+        other = jnp.where(late(inner, outer, 3 + k), jnp.zeros_like(other), other)
         value = value + dot_nn(other, ends[k][...])
     out[...] = value
 
@@ -413,8 +417,8 @@
             [VMEM],
             (gain_smooth,),
             "base_powers",
-            flops=1,
-            size=1,
+            flops=60 * n**3,
+            size=24 * n * n,
         )
 
     aside = []
@@ -459,10 +463,10 @@
 
         def work():
             base_powers = base_work()
-            pi_odd, offset_map = maps(False, (phi, even), loaded, obs, gain, base_powers)
-            return base_powers, pi_odd, offset_map
-
-        other, (base_powers, pi_odd, offsets) = exchange(own_maps[1], "inner", 3, work)
+            pi_odd, odd = maps(False, (phi,), loaded, obs, gain, base_powers)
+            return base_powers, pi_odd, odd
+
+        other, (base_powers, pi_odd, odd) = exchange(own_maps[1], "inner", 3, work)
         other_maps.append(other)
         own_maps.append(total_call(1, place, own_maps[1], other))
     with jax.named_scope("join_2"):
@@ -474,12 +478,23 @@
                 [VMEM],
                 (base_powers,),
                 "high_powers",
-                flops=1,
-                size=1,
+                flops=72 * n**3,
+                size=28 * n * n,
             )
 
+        other = partner(own_maps[2], "inner", 4)
+        offsets = kernel_call(
+            offset_map_body,
+            (n + PAD, n),
+            [VMEM] * 3,
+            (even, odd, base_powers),
+            "offset_map",
+            scratch=[pltpu.VMEM((4, n + PAD, n), F32)],
+            flops=84 * n**3,
+            size=36 * n * n,
+        )
         far = partner(offsets, "inner", 1)
-        other, high = exchange(own_maps[2], "inner", 4, work)
+        other, high, offsets_done = lax.optimization_barrier((other, work(), offsets))
         other_maps.append(other)
         own_maps.append(total_call(2, place, own_maps[2], other))
     with jax.named_scope("join_3"):
@@ -499,10 +514,6 @@
     with jax.named_scope("join_z"):
         chip_map = partner(own_maps[5], "outer", 2)
         inside(0, other_maps[0], through)
-        far, _ = lax.optimization_barrier((far, own_maps[5]))
-        through, offsets = offsets_join(1, own_maps[1], other_maps[1], offsets, far)
-        far = partner(offsets, "inner", 4)
-        inside(1, other_maps[1], through)
         chip_map, aside[:] = lax.optimization_barrier((chip_map, aside))
         total = total_call(5, place, own_maps[5], chip_map)
 
@@ -518,8 +529,8 @@
         y = hop(0, place, first, first, total)
         arrived = lax.ppermute(y, "outer", mirror(0, 1))
         far, _ = lax.optimization_barrier((far, y))
-        through, offsets = offsets_join(2, own_maps[2], other_maps[2], offsets, far)
-        far = partner(offsets, "inner", 12)
+        through, offsets = offsets_join(1, own_maps[1], other_maps[1], offsets, far)
+        far = partner(offsets, "inner", 4)
         arrived, through = lax.optimization_barrier((arrived, through))
     with jax.named_scope("hop_1"):
         y = hop(1, place, first, arrived, total)
@@ -530,15 +541,14 @@
         entry_map = kernel_call(
             entry_map_body,
             (n + PAD, n),
-            [SMEM] * 2 + [VMEM] * 2,
-            (*place, twin, chip_map),
+            [SMEM] * 2 + [VMEM] * 3,
+            (*place, other_maps[3], twin, chip_map),
             "entry_map",
             flops=1,
             size=1,
         )
-        inside(2, other_maps[2], through)
-        far, _ = lax.optimization_barrier((far, y))
-        through, offsets = offsets_join(3, own_maps[3], other_maps[3], offsets, far)
+        inside(1, other_maps[1], through)
+        through, offsets = offsets_join(2, own_maps[2], other_maps[2], offsets, far)
         near, farther, offsets, entry_map, aside[:] = lax.optimization_barrier(
             (near, farther, offsets, entry_map, aside)
         )
@@ -565,22 +575,27 @@
         )
 
     others = []
+    with jax.named_scope("spread_x"):
+        other = partner(value, "inner", 12)
+        inside(2, other_maps[2], through)
+        other, aside[:] = lax.optimization_barrier((other, aside))
+        others.append(other)
+        value = spread(3, value, other)
     with jax.named_scope("spread_core"):
         others.append(partner(value, "outer", 1))
-        value = spread(4, value, others[0])
+        value = spread(4, value, others[1])
     with jax.named_scope("spread_z0"):
         other = partner(value, "outer", 2)
-        inside(3, other_maps[3], through)
         ends = kernel_call(
             ends_body,
-            [(n, n)] * 4,
+            [(n, n)] * 5,
             [SMEM] * 2 + [VMEM] * 3,
             (*place, aside[2], base_powers, high),
             "ends",
-            flops=1,
-            size=1,
-        )
-        other, ends, aside[:] = lax.optimization_barrier((other, ends, aside))
+            flops=60 * n**3,
+            size=36 * n * n,
+        )
+        other, ends = lax.optimization_barrier((other, ends))
         others.append(other)
         value = spread(5, value, other)
     with jax.named_scope("spread_z1"):
@@ -591,8 +606,8 @@
             [VMEM] * 6,
             (entry, aside[0], pi_even, pi_odd, obs, gain),
             "states",
-            flops=1,
-            size=1,
+            flops=17 * 96 * n * n,
+            size=68 * n * n,
         )
         other, pred = lax.optimization_barrier((other, pred))
         others.append(other)
@@ -606,17 +621,17 @@
             (pred, filt, base_powers),
             "local",
             scratch=[pltpu.VMEM((2 * steps, n), F32)],
-            flops=1,
-            size=1,
+            flops=8 * 96 * n * n,
+            size=16 * n * n,
         )
         back = kernel_call(
             gather_body,
             (PAD, n),
-            [SMEM] * 2 + [VMEM] * 9,
-            (*place, entry, aside[1], base_powers, *others, *ends[:3]),
+            [SMEM] * 2 + [VMEM] * 11,
+            (*place, entry, aside[1], base_powers, *others, *ends[:4]),
             "gather",
-            flops=1,
-            size=1,
+            flops=600 * n * n,
+            size=20 * n * n,
         )
         other, base, back = lax.optimization_barrier((other, base, back))
     with jax.named_scope("backward"):
@@ -624,7 +639,7 @@
             backward_body,
             (steps, n),
             [SMEM] * 2 + [VMEM] * 5,
-            (*place, other, ends[3], back, base_powers, base),
+            (*place, other, ends[4], back, base_powers, base),
             "backward",
             flops=600 * n * n,
             size=24 * n * n,

time: 108 us -> 101 us (0.935)
  waiting for transfers between devices: 15.9 us -> 12.5 us
  starting transfers between devices: 43.1 us -> 39.9 us
    ppermute x3 -> x2, waiting for transfers between devices: 2.74 us -> 0.17 us  [exchange(): lax.ppermute(total, axis, [(i, i ^ flip) for i in range(counts[axis])])]
    ppermute x11 -> x12, starting transfers between devices: 27.1 us -> 25.5 us  [partner(): lax.ppermute(value, axis, [(i, i ^ flip) for i in range(counts[axis])])]
    ppermute x3 -> x2, starting transfers between devices: 7.59 us -> 6.3 us  [exchange(): lax.ppermute(total, axis, [(i, i ^ flip) for i in range(counts[axis])])]
    ppermute x11 -> x12, waiting for transfers between devices: 13.1 us -> 12.3 us  [partner(): lax.ppermute(value, axis, [(i, i ^ flip) for i in range(counts[axis])])]
  transfers between devices with their start and end apart: 18 -> 18, of which waited for: 7 -> 9; matrix products, arithmetic and copies ran while one was open for 0% -> 0% of each run, Pallas kernels for 29% -> 30%
where the time goes in v1:
time: 101 us; the launch traced here: 99.6 us
  Pallas kernels  44.8 us (44%)
  starting transfers between devices  39.9 us (40%)
  waiting for transfers between devices  12.5 us (12%)
  local copies, waits for them, and re-layouts  1.4 us (1%)
    pallas_call x31, Pallas kernels, kernel_call(): pl.pallas_call(body, out_shape=shapes, in_specs=in_specs, out_specs=out_s...  44.8 us
    ppermute x12, starting transfers between devices, partner(): lax.ppermute(value, axis, [(i, i ^ flip) for i in range(counts[axis])])  25.5 us
    ppermute x12, waiting for transfers between devices, partner(): lax.ppermute(value, axis, [(i, i ^ flip) for i in range(counts[axis])])  12.3 us
    ppermute x2, starting transfers between devices, exchange(): lax.ppermute(total, axis, [(i, i ^ flip) for i in range(counts[axis])])  6.3 us
    ppermute x1, starting transfers between devices, shards(): arrived = lax.ppermute(y, 'outer', mirror(0, 1))  5.87 us
  transfers between devices with their start and end apart: 18, of which 9 were waited for; matrix products, arithmetic and copies ran while one was open for 0% of the time, Pallas kernels for 30%

profile of v1, /device:TPU:1, one launch (start us, length us, event | category | flops | bytes accessed | tf_op | source)
XLA Modules:
  0.0 99.6 jit_solution(9970610215215031756)
XLA Ops:
  2.0 9.2 %local_map.1 = (f32[264,256]{1,0:T(8,128)S(1)}, f32[264,256]{1,0:T(8,128)S(1)}, f32[264,256]{1,0:T(8,128)S(1)}, f32[264,256]{1,0:T(8,128)S(1)}, f32[16,256,256]{2,1,0:T(8,128)S(1)}) custom-call(s32[1]{0:T(128)} %bitcast.2.inner, s32[1]{0:T(128)} %bitcast.outer, f32[16,256,256]{2,1,0:T(8,128)} %jac_hbm.1, f32[16,256]{1,0:T(8,128)S(1)} %copy-done, ...), custom_call_target="tpu_custom_call" | custom-call | flops 3221225472 | bytes 4194304 | tf_op jit(solution)/shard_map/compose/local_map/pallas_call | solution.py:33
  11.3 2.2 %collective-permute-start = (f32[264,256]{1,0:T(8,128)S(1)}, f32[264,256]{1,0:T(8,128)S(1)}, u32[]{:S(2)}, u32[]{:S(2)}) collective-permute-start(f32[264,256]{1,0:T(8,128)S(1)} %get-tuple-element.78.own.own_map), channel_id=1, source_target_pairs={{0,16},{16,0},{32,48},{48,32},{64,80},{80,64},{96,112},{112,96},{1... | collective-permute-start | bytes 811016 | tf_op jit(solution)/shard_map/join_0/ppermute | solution.py:405
  13.5 4.8 %maps.2 = (f32[8,264,256]{2,1,0:T(8,128)S(1)}, f32[4,264,256]{2,1,0:T(8,128)S(1)}, f32[4,264,256]{2,1,0:T(8,128)S(1)}) custom-call(f32[264,256]{1,0:T(8,128)S(1)} %get-tuple-element.79.refs_0_, f32[264,256]{1,0:T(8,128)S(1)} %get-tuple-element.80.refs_1_, f32[264,256]{1,0:T(8,128)S(1)} %get-tuple-element.81.refs_2_, ...), custom_call_target="tpu_custom_call" | custom-call | flops 1610612736 | bytes 6291456 | tf_op jit(solution)/shard_map/join_0/maps/pallas_call | solution.py:33
  18.9 4.1 %collective-permute-start.1 = (f32[264,256]{1,0:T(8,128)S(1)}, f32[264,256]{1,0:T(8,128)S(1)}, u32[]{:S(2)}, u32[]{:S(2)}) collective-permute-start(f32[264,256]{1,0:T(8,128)S(1)} %total.6.own.own_map), channel_id=1, source_target_pairs={{0,48},{16,32},{32,16},{48,0},{64,112},{80,96},{96,80},{112,64},{1... | collective-permute-start | bytes 811016 | tf_op jit(solution)/shard_map/join_1/ppermute | solution.py:405
  22.9 1.7 %base_powers.1.refs_4_ = f32[5,256,256]{2,1,0:T(8,128)S(1)} custom-call(f32[256,256]{1,0:T(8,128)S(1)} %copy-done.4), custom_call_target="tpu_custom_call" | custom-call | flops 1006632960 | bytes 1572864 | tf_op jit(solution)/shard_map/join_1/base_powers/pallas_call | solution.py:33
  24.7 4.0 %maps.3 = (f32[8,264,256]{2,1,0:T(8,128)S(1)}, f32[4,264,256]{2,1,0:T(8,128)S(1)}) custom-call(f32[4,264,256]{2,1,0:T(8,128)S(1)} %get-tuple-element.87.refs_0_, f32[16,256,256]{2,1,0:T(8,128)S(1)} %get-tuple-element.82.refs_3_.refs_1_, f32[16,256]{1,0:T(8,128)S(1)} %copy-done, f32[1,256]{1,0:T(1,128)S(1)} %bitcast.10, f32[5,256,256]{2,1,0:T(8,128)S(1)} %base_powers.1.refs_4_), custom_call_target="tpu_custom_call" | custom-call | flops 1610612736 | bytes 6291456 | tf_op jit(solution)/shard_map/join_1/maps/pallas_call | solution.py:33
  29.1 1.3 %collective-permute-start.2 = (f32[264,256]{1,0:T(8,128)S(1)}, f32[264,256]{1,0:T(8,128)S(1)}, u32[]{:S(2)}, u32[]{:S(2)}) collective-permute-start(f32[264,256]{1,0:T(8,128)S(1)} %total.7.own.own_map), channel_id=1, source_target_pairs={{0,64},{16,80},{32,96},{48,112},{64,0},{80,16},{96,32},{112,48},{1... | collective-permute-start | bytes 811016 | tf_op jit(solution)/shard_map/join_2/ppermute | solution.py:450
  30.4 2.8 %offset_map.1.own = f32[264,256]{1,0:T(8,128)S(1)} custom-call(f32[4,264,256]{2,1,0:T(8,128)S(1)} %get-tuple-element.92.even, f32[4,264,256]{2,1,0:T(8,128)S(1)} %get-tuple-element.93.odd, f32[5,256,256]{2,1,0:T(8,128)S(1)} %base_powers.1.refs_4_), custom_call_target="tpu_custom_call" | custom-call | flops 1409286144 | bytes 2359296 | tf_op jit(solution)/shard_map/join_2/offset_map/pallas_call | solution.py:33
  33.3 2.4 %high_powers.1.high = f32[7,256,256]{2,1,0:T(8,128)S(1)} custom-call(f32[5,256,256]{2,1,0:T(8,128)S(1)} %base_powers.1.refs_4_), custom_call_target="tpu_custom_call" | custom-call | flops 1207959552 | bytes 1835008 | tf_op jit(solution)/shard_map/join_2/high_powers/pallas_call | solution.py:33
  36.1 2.2 %collective-permute-start.3 = (f32[264,256]{1,0:T(8,128)S(1)}, f32[264,256]{1,0:T(8,128)S(1)}, u32[]{:S(2)}, u32[]{:S(2)}) collective-permute-start(f32[264,256]{1,0:T(8,128)S(1)} %total.8.own), channel_id=1, source_target_pairs={{0,192},{16,208},{32,224},{48,240},{64,128},{80,144},{96,160},{112... | collective-permute-start | bytes 811016 | tf_op jit(solution)/shard_map/join_3/ppermute | solution.py:450
  40.2 2.5 %collective-permute-done.3.other.row_map = f32[264,256]{1,0:T(8,128)S(1)} collective-permute-done((f32[264,256]{1,0:T(8,128)S(1)}, f32[264,256]{1,0:T(8,128)S(1)}, u32[]{:S(2)}, u32[]{:S(2)}) %collective-permute-start.3) | collective-permute-done | bytes 270368 | tf_op jit(solution)/shard_map/join_3/ppermute | solution.py:450
  43.1 3.7 %collective-permute-start.5 = (f32[264,256]{1,0:T(8,128)S(1)}, f32[264,256]{1,0:T(8,128)S(1)}, u32[]{:S(2)}, u32[]{:S(2)}) collective-permute-start(f32[264,256]{1,0:T(8,128)S(1)} %total.9.own), channel_id=1, source_target_pairs={{0,1},{1,0},{2,3},{3,2},{4,5},{5,4},{6,7},{7,6},{8,9},{9,8},{10,11... | collective-permute-start | bytes 811016 | tf_op jit(solution)/shard_map/join_core/ppermute | solution.py:450
  48.4 1.7 %collective-permute-start.6 = (f32[264,256]{1,0:T(8,128)S(1)}, f32[264,256]{1,0:T(8,128)S(1)}, u32[]{:S(2)}, u32[]{:S(2)}) collective-permute-start(f32[264,256]{1,0:T(8,128)S(1)} %total.10.own), channel_id=1, source_target_pairs={{0,2},{1,3},{2,0},{3,1},{4,6},{5,7},{6,4},{7,5},{8,10},{9,11},{10,... | collective-permute-start | bytes 811016 | tf_op jit(solution)/shard_map/join_z/ppermute | solution.py:450
  50.1 2.2 %collective-permute-start.8 = (f32[264,256]{1,0:T(8,128)S(1)}, f32[264,256]{1,0:T(8,128)S(1)}, u32[]{:S(2)}, u32[]{:S(2)}) collective-permute-start(f32[264,256]{1,0:T(8,128)S(1)} %get-tuple-element.103.own), channel_id=1, source_target_pairs={{0,48},{16,32},{32,16},{48,0},{64,112},{80,96},{96,80},{112,64},{1... | collective-permute-start | bytes 811016 | tf_op jit(solution)/shard_map/join_3/ppermute | solution.py:450
  52.4 4.1 %collective-permute-done.6.other.chip_map = f32[264,256]{1,0:T(8,128)S(1)} collective-permute-done((f32[264,256]{1,0:T(8,128)S(1)}, f32[264,256]{1,0:T(8,128)S(1)}, u32[]{:S(2)}, u32[]{:S(2)}) %collective-permute-start.6) | collective-permute-done | bytes 270368 | tf_op jit(solution)/shard_map/join_z/ppermute | solution.py:450
  57.2 5.9 %collective-permute-start.7 = (f32[8,256]{1,0:T(8,128)S(1)}, f32[8,256]{1,0:T(8,128)S(1)}, u32[]{:S(2)}, u32[]{:S(2)}) collective-permute-start(f32[8,256]{1,0:T(8,128)S(1)} %hop.2), channel_id=1, source_target_pairs={{0,6},{1,7},{2,4},{3,5},{16,22},{17,23},{18,20},{19,21},{32,38},{3... | collective-permute-start | bytes 24584 | tf_op jit(solution)/shard_map/hop_0/ppermute | solution.py:530
  68.6 2.1 %collective-permute-done.11.other = f32[264,256]{1,0:T(8,128)S(1)} collective-permute-done((f32[264,256]{1,0:T(8,128)S(1)}, f32[264,256]{1,0:T(8,128)S(1)}, u32[]{:S(2)}, u32[]{:S(2)}) %collective-permute-start.11) | collective-permute-done | bytes 270368 | tf_op jit(solution)/shard_map/hop_0/ppermute | solution.py:450
  72.6 2.4 %collective-permute-start.13 = (f32[8,256]{1,0:T(8,128)S(1)}, f32[8,256]{1,0:T(8,128)S(1)}, u32[]{:S(2)}, u32[]{:S(2)}) collective-permute-start(f32[8,256]{1,0:T(8,128)S(1)} %get-tuple-element.122.own), channel_id=1, source_target_pairs={{0,192},{16,208},{32,224},{48,240},{64,128},{80,144},{96,160},{112... | collective-permute-start | bytes 24584 | tf_op jit(solution)/shard_map/spread_x/ppermute | solution.py:450
  76.5 3.6 %collective-permute-start.14 = (f32[8,256]{1,0:T(8,128)S(1)}, f32[8,256]{1,0:T(8,128)S(1)}, u32[]{:S(2)}, u32[]{:S(2)}) collective-permute-start(f32[8,256]{1,0:T(8,128)S(1)} %spread.4.own), channel_id=1, source_target_pairs={{0,1},{1,0},{2,3},{3,2},{4,5},{5,4},{6,7},{7,6},{8,9},{9,8},{10,11... | collective-permute-start | bytes 24584 | tf_op jit(solution)/shard_map/spread_core/ppermute | solution.py:450
  81.1 2.2 %ends.1 = (f32[256,256]{1,0:T(8,128)S(1)}, f32[256,256]{1,0:T(8,128)S(1)}, f32[256,256]{1,0:T(8,128)S(1)}, f32[256,256]{1,0:T(8,128)S(1)}, f32[256,256]{1,0:T(8,128)S(1)}) custom-call(s32[1]{0:T(128)} %bitcast.2.inner, s32[1]{0:T(128)} %bitcast.outer, f32[256,256]{1,0:T(8,128)S(1)} %get-tuple-element.135.lift, f32[5,256,256]{2,1,0:T(8,128)S(1)} %base_powers.1.refs_4_, ...), custom_call_target="tpu_custom_call" | custom-call | flops 1006632960 | bytes 2359296 | tf_op jit(solution)/shard_map/spread_z0/ends/pallas_call | solution.py:33
  83.9 3.9 %collective-permute-start.16 = (f32[8,256]{1,0:T(8,128)S(1)}, f32[8,256]{1,0:T(8,128)S(1)}, u32[]{:S(2)}, u32[]{:S(2)}) collective-permute-start(f32[8,256]{1,0:T(8,128)S(1)} %spread.6.own), channel_id=1, source_target_pairs={{0,4},{1,5},{2,6},{3,7},{4,0},{5,1},{6,2},{7,3},{8,12},{9,13},{10,... | collective-permute-start | bytes 24584 | tf_op jit(solution)/shard_map/spread_z1/ppermute | solution.py:450
  87.7 3.2 %states.1 = (f32[16,256]{1,0:T(8,128)S(1)}, f32[16,256]{1,0:T(8,128)}) custom-call(f32[8,256]{1,0:T(8,128)S(1)} %get-tuple-element.121.entry, f32[264,256]{1,0:T(8,128)S(1)} %get-tuple-element.130.before, f32[8,264,256]{2,1,0:T(8,128)S(1)} %get-tuple-element.131.even, f32[8,264,256]{2,1,0:T(8,128)S(1)} %get-tuple-element.132.odd, f32[16,256]{1,0:T(8,128)S(1)} %copy-done, ...), custom_call_target="tpu_custom_call" | custom-call | flops 106954752 | bytes 4456448 | tf_op jit(solution)/shard_map/spread_z1/states/pallas_call | solution.py:33
  91.2 4.4 %collective-permute-start.17 = (f32[8,256]{1,0:T(8,128)S(1)}, f32[8,256]{1,0:T(8,128)S(1)}, u32[]{:S(2)}, u32[]{:S(2)}) collective-permute-start(f32[8,256]{1,0:T(8,128)S(1)} %spread.7), channel_id=1, source_target_pairs={{0,14},{1,15},{2,12},{3,13},{4,10},{5,11},{6,8},{7,9},{8,6},{9,7},... | collective-permute-start | bytes 24584 | tf_op jit(solution)/shard_map/spread_z2/ppermute | solution.py:450
  97.6 2.0 %backward.1 = f32[16,256]{1,0:T(8,128)} custom-call(s32[1]{0:T(128)} %bitcast.2.inner, s32[1]{0:T(128)} %bitcast.outer, f32[8,256]{1,0:T(8,128)S(1)} %collective-permute-done.17.other, f32[256,256]{1,0:T(8,128)S(1)} %get-tuple-element.151.end, f32[8,256]{1,0:T(8,128)S(1)} %gather.1.back, f32[5,256,256]{2,1,0:T(8,128)S(1)} %base_powers.1.refs_4_, ...), custom_call_target="tpu_custom_call" | custom-call | flops 39321600 | bytes 1572864 | tf_op jit(solution)/shard_map/backward/backward/pallas_call | solution.py:33
  (53 shorter events, 20.2 us)
Async XLA Ops:
  0.6 0.7 copy-start
  1.4 0.7 copy-start.3
  2.0 11.4 %copy-start.4 = (f32[256,256]{1,0:T(8,128)S(1)}, f32[256,256]{1,0:T(8,128)}, u32[]{:S(2)}) copy-start(f32[256,256]{1,0:T(8,128)} %smooth.1) | copy-start | bytes 786436
  11.3 7.2 %collective-permute-start = (f32[264,256]{1,0:T(8,128)S(1)}, f32[264,256]{1,0:T(8,128)S(1)}, u32[]{:S(2)}, u32[]{:S(2)}) collective-permute-start(f32[264,256]{1,0:T(8,128)S(1)} %get-tuple-element.78.own.own_map), channel_id=1, source_target_pairs={{0,16},{16,0},{32,48},{48,32},{64,80},{80,64},{96,112},{112,96},{1... | collective-permute-start | bytes 811016 | tf_op jit(solution)/shard_map/join_0/ppermute | solution.py:405
  18.9 9.8 %collective-permute-start.1 = (f32[264,256]{1,0:T(8,128)S(1)}, f32[264,256]{1,0:T(8,128)S(1)}, u32[]{:S(2)}, u32[]{:S(2)}) collective-permute-start(f32[264,256]{1,0:T(8,128)S(1)} %total.6.own.own_map), channel_id=1, source_target_pairs={{0,48},{16,32},{32,16},{48,0},{64,112},{80,96},{96,80},{112,64},{1... | collective-permute-start | bytes 811016 | tf_op jit(solution)/shard_map/join_1/ppermute | solution.py:405
  29.1 6.6 %collective-permute-start.2 = (f32[264,256]{1,0:T(8,128)S(1)}, f32[264,256]{1,0:T(8,128)S(1)}, u32[]{:S(2)}, u32[]{:S(2)}) collective-permute-start(f32[264,256]{1,0:T(8,128)S(1)} %total.7.own.own_map), channel_id=1, source_target_pairs={{0,64},{16,80},{32,96},{48,112},{64,0},{80,16},{96,32},{112,48},{1... | collective-permute-start | bytes 811016 | tf_op jit(solution)/shard_map/join_2/ppermute | solution.py:450
  33.2 6.0 %collective-permute-start.4 = (f32[264,256]{1,0:T(8,128)S(1)}, f32[264,256]{1,0:T(8,128)S(1)}, u32[]{:S(2)}, u32[]{:S(2)}) collective-permute-start(f32[264,256]{1,0:T(8,128)S(1)} %offset_map.1.own), channel_id=1, source_target_pairs={{0,16},{16,0},{32,48},{48,32},{64,80},{80,64},{96,112},{112,96},{1... | collective-permute-start | bytes 811016 | tf_op jit(solution)/shard_map/join_2/ppermute | solution.py:450
  36.1 6.6 %collective-permute-start.3 = (f32[264,256]{1,0:T(8,128)S(1)}, f32[264,256]{1,0:T(8,128)S(1)}, u32[]{:S(2)}, u32[]{:S(2)}) collective-permute-start(f32[264,256]{1,0:T(8,128)S(1)} %total.8.own), channel_id=1, source_target_pairs={{0,192},{16,208},{32,224},{48,240},{64,128},{80,144},{96,160},{112... | collective-permute-start | bytes 811016 | tf_op jit(solution)/shard_map/join_3/ppermute | solution.py:450
  43.1 13.8 %copy-start.2 = (f32[256]{0:T(256)S(1)}, f32[256]{0:T(256)}, u32[]{:S(2)}) copy-start(f32[256]{0:T(256)} %param.9) | copy-start | bytes 3076
  43.1 4.8 %collective-permute-start.5 = (f32[264,256]{1,0:T(8,128)S(1)}, f32[264,256]{1,0:T(8,128)S(1)}, u32[]{:S(2)}, u32[]{:S(2)}) collective-permute-start(f32[264,256]{1,0:T(8,128)S(1)} %total.9.own), channel_id=1, source_target_pairs={{0,1},{1,0},{2,3},{3,2},{4,5},{5,4},{6,7},{7,6},{8,9},{9,8},{10,11... | collective-permute-start | bytes 811016 | tf_op jit(solution)/shard_map/join_core/ppermute | solution.py:450
  48.4 8.1 %collective-permute-start.6 = (f32[264,256]{1,0:T(8,128)S(1)}, f32[264,256]{1,0:T(8,128)S(1)}, u32[]{:S(2)}, u32[]{:S(2)}) collective-permute-start(f32[264,256]{1,0:T(8,128)S(1)} %total.10.own), channel_id=1, source_target_pairs={{0,2},{1,3},{2,0},{3,1},{4,6},{5,7},{6,4},{7,5},{8,10},{9,11},{10,... | collective-permute-start | bytes 811016 | tf_op jit(solution)/shard_map/join_z/ppermute | solution.py:450
  50.1 12.9 %collective-permute-start.8 = (f32[264,256]{1,0:T(8,128)S(1)}, f32[264,256]{1,0:T(8,128)S(1)}, u32[]{:S(2)}, u32[]{:S(2)}) collective-permute-start(f32[264,256]{1,0:T(8,128)S(1)} %get-tuple-element.103.own), channel_id=1, source_target_pairs={{0,48},{16,32},{32,16},{48,0},{64,112},{80,96},{96,80},{112,64},{1... | collective-permute-start | bytes 811016 | tf_op jit(solution)/shard_map/join_3/ppermute | solution.py:450
  57.2 7.1 %collective-permute-start.7 = (f32[8,256]{1,0:T(8,128)S(1)}, f32[8,256]{1,0:T(8,128)S(1)}, u32[]{:S(2)}, u32[]{:S(2)}) collective-permute-start(f32[8,256]{1,0:T(8,128)S(1)} %hop.2), channel_id=1, source_target_pairs={{0,6},{1,7},{2,4},{3,5},{16,22},{17,23},{18,20},{19,21},{32,38},{3... | collective-permute-start | bytes 24584 | tf_op jit(solution)/shard_map/hop_0/ppermute | solution.py:530
  64.1 6.6 %collective-permute-start.11 = (f32[264,256]{1,0:T(8,128)S(1)}, f32[264,256]{1,0:T(8,128)S(1)}, u32[]{:S(2)}, u32[]{:S(2)}) collective-permute-start(f32[264,256]{1,0:T(8,128)S(1)} %get-tuple-element.107.own), channel_id=1, source_target_pairs={{0,64},{16,80},{32,96},{48,112},{64,0},{80,16},{96,32},{112,48},{1... | collective-permute-start | bytes 811016 | tf_op jit(solution)/shard_map/hop_0/ppermute | solution.py:450
  64.4 7.3 %collective-permute-start.12 = (f32[264,256]{1,0:T(8,128)S(1)}, f32[264,256]{1,0:T(8,128)S(1)}, u32[]{:S(2)}, u32[]{:S(2)}) collective-permute-start(f32[264,256]{1,0:T(8,128)S(1)} %total.11.group_map), channel_id=1, source_target_pairs={{8,14},{9,15},{10,12},{11,13},{24,30},{25,31},{26,28},{27,29},{40,... | collective-permute-start | bytes 811016 | tf_op jit(solution)/shard_map/hop_1/ppermute | solution.py:540
  65.3 6.4 %collective-permute-start.10 = (f32[8,256]{1,0:T(8,128)S(1)}, f32[8,256]{1,0:T(8,128)S(1)}, u32[]{:S(2)}, u32[]{:S(2)}) collective-permute-start(f32[8,256]{1,0:T(8,128)S(1)} %hop.3), channel_id=1, source_target_pairs={{4,14},{5,15},{6,12},{7,13},{20,30},{21,31},{22,28},{23,29},{36,46... | collective-permute-start | bytes 24584 | tf_op jit(solution)/shard_map/hop_1/ppermute | solution.py:538
  66.0 5.8 %collective-permute-start.9 = (f32[8,256]{1,0:T(8,128)S(1)}, f32[8,256]{1,0:T(8,128)S(1)}, u32[]{:S(2)}, u32[]{:S(2)}) collective-permute-start(f32[8,256]{1,0:T(8,128)S(1)} %hop.3), channel_id=1, source_target_pairs={{4,10},{5,11},{6,8},{7,9},{20,26},{21,27},{22,24},{23,25},{36,42},... | collective-permute-start | bytes 24584 | tf_op jit(solution)/shard_map/hop_1/ppermute | solution.py:537
  72.6 3.7 %collective-permute-start.13 = (f32[8,256]{1,0:T(8,128)S(1)}, f32[8,256]{1,0:T(8,128)S(1)}, u32[]{:S(2)}, u32[]{:S(2)}) collective-permute-start(f32[8,256]{1,0:T(8,128)S(1)} %get-tuple-element.122.own), channel_id=1, source_target_pairs={{0,192},{16,208},{32,224},{48,240},{64,128},{80,144},{96,160},{112... | collective-permute-start | bytes 24584 | tf_op jit(solution)/shard_map/spread_x/ppermute | solution.py:450
  76.5 4.4 %collective-permute-start.14 = (f32[8,256]{1,0:T(8,128)S(1)}, f32[8,256]{1,0:T(8,128)S(1)}, u32[]{:S(2)}, u32[]{:S(2)}) collective-permute-start(f32[8,256]{1,0:T(8,128)S(1)} %spread.4.own), channel_id=1, source_target_pairs={{0,1},{1,0},{2,3},{3,2},{4,5},{5,4},{6,7},{7,6},{8,9},{9,8},{10,11... | collective-permute-start | bytes 24584 | tf_op jit(solution)/shard_map/spread_core/ppermute | solution.py:450
  81.1 2.5 %collective-permute-start.15 = (f32[8,256]{1,0:T(8,128)S(1)}, f32[8,256]{1,0:T(8,128)S(1)}, u32[]{:S(2)}, u32[]{:S(2)}) collective-permute-start(f32[8,256]{1,0:T(8,128)S(1)} %spread.5.own), channel_id=1, source_target_pairs={{0,2},{1,3},{2,0},{3,1},{4,6},{5,7},{6,4},{7,5},{8,10},{9,11},{10,... | collective-permute-start | bytes 24584 | tf_op jit(solution)/shard_map/spread_z0/ppermute | solution.py:450
  83.9 7.1 %collective-permute-start.16 = (f32[8,256]{1,0:T(8,128)S(1)}, f32[8,256]{1,0:T(8,128)S(1)}, u32[]{:S(2)}, u32[]{:S(2)}) collective-permute-start(f32[8,256]{1,0:T(8,128)S(1)} %spread.6.own), channel_id=1, source_target_pairs={{0,4},{1,5},{2,6},{3,7},{4,0},{5,1},{6,2},{7,3},{8,12},{9,13},{10,... | collective-permute-start | bytes 24584 | tf_op jit(solution)/shard_map/spread_z1/ppermute | solution.py:450
  91.0 5.4 %copy-start.1 = (f32[16,256]{1,0:T(8,128)S(1)}, f32[16,256]{1,0:T(8,128)}, u32[]{:S(2)}) copy-start(f32[16,256]{1,0:T(8,128)} %get-tuple-element.76.filt) | copy-start | bytes 49156
  91.2 6.4 %collective-permute-start.17 = (f32[8,256]{1,0:T(8,128)S(1)}, f32[8,256]{1,0:T(8,128)S(1)}, u32[]{:S(2)}, u32[]{:S(2)}) collective-permute-start(f32[8,256]{1,0:T(8,128)S(1)} %spread.7), channel_id=1, source_target_pairs={{0,14},{1,15},{2,12},{3,13},{4,10},{5,11},{6,8},{7,9},{8,6},{9,7},... | collective-permute-start | bytes 24584 | tf_op jit(solution)/shard_map/spread_z2/ppermute | solution.py:450

commit v2 on v1

--- a/solution.py
+++ b/solution.py
@@ -272,30 +272,28 @@
     out[...] = jnp.where(is_late, other[...], own[...]) + dot_nn(through[...], high[level])
 
 
-def inside_body(level, inner, outer, other_map, through, high, *refs):
-    before_out, behind_out, lift_out = refs[-3:]
-    n = high.shape[2]
+def inside_body(level, inner, outer, other_map, through, ends, *refs):
+    before_out, behind_out = refs[-2:]
+    n = ends.shape[2]
     is_late = late(inner, outer, level)
     if level == 0:
         row = lax.broadcasted_iota(jnp.int32, (n + PAD, n), 0)
         column = lax.broadcasted_iota(jnp.int32, (n + PAD, n), 1)
         eye = jnp.where(row == column, 1.0, 0.0).astype(F32)
         before_out[...] = jnp.where(is_late, other_map[...], eye)
-        behind_out[...] = jnp.where(is_late, jnp.zeros_like(eye), through[...])
-        lift_out[...] = jnp.where(is_late, eye[:n], high[level])
+        moved = dot_nn(through[...], ends[0])
+        behind_out[...] = jnp.where(is_late, jnp.zeros_like(moved), moved)
         return
-    before, behind, lift = refs[:3]
+    before, behind = refs[:2]
     first = jnp.where(is_late, other_map[...], through[...])
-    moved = dot_nn(first, jnp.where(is_late, behind[:n], lift[...]))
+    moved = dot_nn(first, jnp.where(is_late, behind[:n], ends[level]))
     kept = behind[...]
     behind_out[:n] = moved[:n] + jnp.where(is_late, jnp.zeros_like(kept[:n]), kept[:n])
     behind_out[n:] = moved[n:] + kept[n:]
-    second = jnp.where(is_late, other_map[:n], lift[...])
-    moved = dot_nn(second, jnp.where(is_late, before[:n], high[level]))
-    edge = dot_nn(other_map[n:], before[:n]) + before[n:]
-    before_out[:n] = jnp.where(is_late, moved, before[:n])
-    before_out[n:] = jnp.where(is_late, edge, before[n:])
-    lift_out[...] = jnp.where(is_late, lift[...], moved)
+    moved = dot_nn(other_map[...], before[:n])
+    kept = before[...]
+    before_out[:n] = jnp.where(is_late, moved[:n], kept[:n])
+    before_out[n:] = jnp.where(is_late, moved[n:] + kept[n:], kept[n:])
 
 
 def entry_map_body(inner, outer, row_map, twin, chip_map, out):
@@ -331,11 +329,11 @@
     out[...] = early_half + dot_nn(late_half, high[level])
 
 
-def ends_body(inner, outer, lift, base_powers, high, *ends):
-    ends[0][...] = dot_nn(lift[...], base_powers[0])
-    for k in range(len(ends) - 1):
-        moved = dot_nn(ends[k][...], high[3 + k])
-        ends[k + 1][...] = jnp.where(late(inner, outer, 3 + k), ends[k][...], moved)
+def ends_body(inner, outer, base_powers, high, ends):
+    ends[0] = base_powers[0]
+    for k in range(ends.shape[0] - 1):
+        moved = dot_nn(ends[k], high[k])
+        ends[k + 1] = jnp.where(late(inner, outer, k), ends[k], moved)
 
 
 def states_body(entry, before, even, odd, obs, gain, pred, filt):
@@ -368,24 +366,24 @@
     base[...] = pred[...] + local
 
 
-def gather_body(inner, outer, entry, behind, base_powers, *refs):
-    count = len(refs) // 2
-    others, ends, out = refs[:count], refs[count : 2 * count], refs[2 * count]
+def gather_body(inner, outer, entry, behind, ends, *refs):
+    others, out = refs[:-1], refs[-1]
     n = entry.shape[1]
-    inside = dot_nn(entry[...], behind[:n]) + behind[n:]
-    value = dot_nn(inside, base_powers[0])
-    for k in range(count):
-        other = others[k][...]
+    value = dot_nn(entry[...], behind[:n]) + behind[n:]
+    for k, ref in enumerate(others):
+        other = ref[...]
         other = jnp.where(late(inner, outer, 3 + k), jnp.zeros_like(other), other)
-        value = value + dot_nn(other, ends[k][...])
+        value = value + dot_nn(other, ends[3 + k])
     out[...] = value
 
 
-def backward_body(inner, outer, other, end, back, base_powers, base, out):
+def backward_body(inner, outer, one, two, ends, back, base_powers, base, out):
     steps, n = base.shape
-    value = other[...]
-    value = jnp.where(late(inner, outer, 7), jnp.zeros_like(value), value)
-    value = back[...] + dot_nn(value, end[...])
+    value = back[...]
+    for level, ref in ((6, one), (7, two)):
+        other = ref[...]
+        other = jnp.where(late(inner, outer, level), jnp.zeros_like(other), other)
+        value = value + dot_nn(other, ends[level])
     left = steps - 1 - lax.broadcasted_iota(jnp.int32, (steps, n), 0)
     value = jnp.concatenate([value, value], 0)
     for level in range(base_powers.shape[0] - 1):
@@ -438,9 +436,9 @@
     def inside(level, other_map, through):
         aside[:] = kernel_call(
             functools.partial(inside_body, level),
-            [(n + PAD, n), (n + PAD, n), (n, n)],
+            [(n + PAD, n), (n + PAD, n)],
             [SMEM] * 2 + [VMEM] * (3 + len(aside)),
-            (*place, other_map, through, high, *aside),
+            (*place, other_map, through, ends, *aside),
             "inside",
             flops=1,
             size=1,
@@ -505,7 +503,16 @@
 
         other = partner(own_maps[3], "inner", 12)
         through, offsets, far = work()
-        other, through = lax.optimization_barrier((other, through))
+        ends = kernel_call(
+            ends_body,
+            (8, n, n),
+            [SMEM] * 2 + [VMEM] * 2,
+            (*place, base_powers, high),
+            "ends",
+            flops=1,
+            size=1,
+        )
+        other, through, ends = lax.optimization_barrier((other, through, ends))
         other_maps.append(other)
         own_maps.append(total_call(3, place, own_maps[3], other))
     with jax.named_scope("join_core"):
@@ -586,34 +593,20 @@
         value = spread(4, value, others[1])
     with jax.named_scope("spread_z0"):
         other = partner(value, "outer", 2)
-        ends = kernel_call(
-            ends_body,
-            [(n, n)] * 5,
-            [SMEM] * 2 + [VMEM] * 3,
-            (*place, aside[2], base_powers, high),
-            "ends",
-            flops=60 * n**3,
-            size=36 * n * n,
-        )
-        other, ends = lax.optimization_barrier((other, ends))
-        others.append(other)
-        value = spread(5, value, other)
-    with jax.named_scope("spread_z1"):
-        other = partner(value, "outer", 4)
         pred, filt = kernel_call(
             states_body,
             [(steps, n), (steps, n)],
             [VMEM] * 6,
             (entry, aside[0], pi_even, pi_odd, obs, gain),
             "states",
-            flops=17 * 96 * n * n,
-            size=68 * n * n,
+            flops=1,
+            size=1,
         )
         other, pred = lax.optimization_barrier((other, pred))
         others.append(other)
-        value = spread(6, value, other)
-    with jax.named_scope("spread_z2"):
-        other = partner(value, "outer", 14)
+        value = spread(5, value, other)
+    with jax.named_scope("spread_z1"):
+        other = partner(value, "outer", 4)
         base = kernel_call(
             local_body,
             (steps, n),
@@ -621,25 +614,29 @@
             (pred, filt, base_powers),
             "local",
             scratch=[pltpu.VMEM((2 * steps, n), F32)],
-            flops=8 * 96 * n * n,
-            size=16 * n * n,
+            flops=1,
+            size=1,
         )
         back = kernel_call(
             gather_body,
             (PAD, n),
-            [SMEM] * 2 + [VMEM] * 11,
-            (*place, entry, aside[1], base_powers, *others, *ends[:4]),
+            [SMEM] * 2 + [VMEM] * 6,
+            (*place, entry, aside[1], ends, *others),
             "gather",
-            flops=600 * n * n,
-            size=20 * n * n,
+            flops=1,
+            size=1,
         )
         other, base, back = lax.optimization_barrier((other, base, back))
+        others.append(other)
+        value = spread(6, value, other)
+    with jax.named_scope("spread_z2"):
+        other = partner(value, "outer", 14)
     with jax.named_scope("backward"):
         smoothed = kernel_call(
             backward_body,
             (steps, n),
-            [SMEM] * 2 + [VMEM] * 5,
-            (*place, other, ends[4], back, base_powers, base),
+            [SMEM] * 2 + [VMEM] * 6,
+            (*place, others[3], other, ends, back, base_powers, base),
             "backward",
             flops=600 * n * n,
             size=24 * n * n,

time: 101 us -> 101 us (level)
  waiting for transfers between devices: 12.5 us -> 10.2 us
  Pallas kernels: 44.8 us -> 45.9 us
    ppermute x12, waiting for transfers between devices: 12.3 us -> 9.99 us  [partner(): lax.ppermute(value, axis, [(i, i ^ flip) for i in range(counts[axis])])]
    pallas_call x31, Pallas kernels: 44.8 us -> 45.9 us  [kernel_call(): pl.pallas_call(body, out_shape=shapes, in_specs=in_specs, out_specs=out_s...]
  transfers between devices with their start and end apart: 18 -> 18, of which waited for: 9 -> 8; matrix products, arithmetic and copies ran while one was open for 0% -> 0% of each run, Pallas kernels for 30% -> 31%
where the time goes in v2:
time: 101 us; the launch traced here: 99.5 us
  Pallas kernels  45.9 us (45%)
  starting transfers between devices  40.4 us (40%)
  waiting for transfers between devices  10.2 us (10%)
  local copies, waits for them, and re-layouts  2.12 us (2%)
    pallas_call x31, Pallas kernels, kernel_call(): pl.pallas_call(body, out_shape=shapes, in_specs=in_specs, out_specs=out_s...  45.9 us
    ppermute x12, starting transfers between devices, partner(): lax.ppermute(value, axis, [(i, i ^ flip) for i in range(counts[axis])])  26.2 us
    ppermute x12, waiting for transfers between devices, partner(): lax.ppermute(value, axis, [(i, i ^ flip) for i in range(counts[axis])])  9.99 us
    ppermute x2, starting transfers between devices, exchange(): lax.ppermute(total, axis, [(i, i ^ flip) for i in range(counts[axis])])  6.3 us
    ppermute x1, starting transfers between devices, shards(): arrived = lax.ppermute(y, 'outer', mirror(0, 1))  5.86 us
    unnamed x10, local copies, waits for them, and re-layouts  2.12 us
  transfers between devices with their start and end apart: 18, of which 8 were waited for; matrix products, arithmetic and copies ran while one was open for 0% of the time, Pallas kernels for 31%

profile of v2, /device:TPU:1, one launch (start us, length us, event | category | flops | bytes accessed | tf_op | source)
XLA Modules:
  0.0 99.5 jit_solution(12561214590416325761)
XLA Ops:
  2.0 9.2 %local_map.1 = (f32[264,256]{1,0:T(8,128)S(1)}, f32[264,256]{1,0:T(8,128)S(1)}, f32[264,256]{1,0:T(8,128)S(1)}, f32[264,256]{1,0:T(8,128)S(1)}, f32[16,256,256]{2,1,0:T(8,128)S(1)}) custom-call(s32[1]{0:T(128)} %bitcast.2.inner, s32[1]{0:T(128)} %bitcast.outer, f32[16,256,256]{2,1,0:T(8,128)} %jac_hbm.1, f32[16,256]{1,0:T(8,128)S(1)} %copy-done, ...), custom_call_target="tpu_custom_call" | custom-call | flops 3221225472 | bytes 4194304 | tf_op jit(solution)/shard_map/compose/local_map/pallas_call | solution.py:33
  11.3 2.2 %collective-permute-start = (f32[264,256]{1,0:T(8,128)S(1)}, f32[264,256]{1,0:T(8,128)S(1)}, u32[]{:S(2)}, u32[]{:S(2)}) collective-permute-start(f32[264,256]{1,0:T(8,128)S(1)} %get-tuple-element.62.own.own_map), channel_id=1, source_target_pairs={{0,16},{16,0},{32,48},{48,32},{64,80},{80,64},{96,112},{112,96},{1... | collective-permute-start | bytes 811016 | tf_op jit(solution)/shard_map/join_0/ppermute | solution.py:403
  13.5 4.8 %maps.2 = (f32[8,264,256]{2,1,0:T(8,128)S(1)}, f32[4,264,256]{2,1,0:T(8,128)S(1)}, f32[4,264,256]{2,1,0:T(8,128)S(1)}) custom-call(f32[264,256]{1,0:T(8,128)S(1)} %get-tuple-element.63.refs_0_, f32[264,256]{1,0:T(8,128)S(1)} %get-tuple-element.64.refs_1_, f32[264,256]{1,0:T(8,128)S(1)} %get-tuple-element.65.refs_2_, ...), custom_call_target="tpu_custom_call" | custom-call | flops 1610612736 | bytes 6291456 | tf_op jit(solution)/shard_map/join_0/maps/pallas_call | solution.py:33
  18.9 4.1 %collective-permute-start.1 = (f32[264,256]{1,0:T(8,128)S(1)}, f32[264,256]{1,0:T(8,128)S(1)}, u32[]{:S(2)}, u32[]{:S(2)}) collective-permute-start(f32[264,256]{1,0:T(8,128)S(1)} %total.6.own.own_map), channel_id=1, source_target_pairs={{0,48},{16,32},{32,16},{48,0},{64,112},{80,96},{96,80},{112,64},{1... | collective-permute-start | bytes 811016 | tf_op jit(solution)/shard_map/join_1/ppermute | solution.py:403
  22.9 1.7 %base_powers.1.refs_4_ = f32[5,256,256]{2,1,0:T(8,128)S(1)} custom-call(f32[256,256]{1,0:T(8,128)S(1)} %copy-done.4), custom_call_target="tpu_custom_call" | custom-call | flops 1006632960 | bytes 1572864 | tf_op jit(solution)/shard_map/join_1/base_powers/pallas_call | solution.py:33
  24.6 4.0 %maps.3 = (f32[8,264,256]{2,1,0:T(8,128)S(1)}, f32[4,264,256]{2,1,0:T(8,128)S(1)}) custom-call(f32[4,264,256]{2,1,0:T(8,128)S(1)} %get-tuple-element.71.refs_0_, f32[16,256,256]{2,1,0:T(8,128)S(1)} %get-tuple-element.66.refs_3_.refs_1_, f32[16,256]{1,0:T(8,128)S(1)} %copy-done, f32[1,256]{1,0:T(1,128)S(1)} %bitcast.10, f32[5,256,256]{2,1,0:T(8,128)S(1)} %base_powers.1.refs_4_), custom_call_target="tpu_custom_call" | custom-call | flops 1610612736 | bytes 6291456 | tf_op jit(solution)/shard_map/join_1/maps/pallas_call | solution.py:33
  29.1 1.3 %collective-permute-start.2 = (f32[264,256]{1,0:T(8,128)S(1)}, f32[264,256]{1,0:T(8,128)S(1)}, u32[]{:S(2)}, u32[]{:S(2)}) collective-permute-start(f32[264,256]{1,0:T(8,128)S(1)} %total.7.own.own_map), channel_id=1, source_target_pairs={{0,64},{16,80},{32,96},{48,112},{64,0},{80,16},{96,32},{112,48},{1... | collective-permute-start | bytes 811016 | tf_op jit(solution)/shard_map/join_2/ppermute | solution.py:448
  30.4 2.8 %offset_map.1.own = f32[264,256]{1,0:T(8,128)S(1)} custom-call(f32[4,264,256]{2,1,0:T(8,128)S(1)} %get-tuple-element.76.even, f32[4,264,256]{2,1,0:T(8,128)S(1)} %get-tuple-element.77.odd, f32[5,256,256]{2,1,0:T(8,128)S(1)} %base_powers.1.refs_4_), custom_call_target="tpu_custom_call" | custom-call | flops 1409286144 | bytes 2359296 | tf_op jit(solution)/shard_map/join_2/offset_map/pallas_call | solution.py:33
  33.3 2.4 %high_powers.1.high = f32[7,256,256]{2,1,0:T(8,128)S(1)} custom-call(f32[5,256,256]{2,1,0:T(8,128)S(1)} %base_powers.1.refs_4_), custom_call_target="tpu_custom_call" | custom-call | flops 1207959552 | bytes 1835008 | tf_op jit(solution)/shard_map/join_2/high_powers/pallas_call | solution.py:33
  36.1 2.2 %collective-permute-start.3 = (f32[264,256]{1,0:T(8,128)S(1)}, f32[264,256]{1,0:T(8,128)S(1)}, u32[]{:S(2)}, u32[]{:S(2)}) collective-permute-start(f32[264,256]{1,0:T(8,128)S(1)} %total.8.own), channel_id=1, source_target_pairs={{0,192},{16,208},{32,224},{48,240},{64,128},{80,144},{96,160},{112... | collective-permute-start | bytes 811016 | tf_op jit(solution)/shard_map/join_3/ppermute | solution.py:448
  38.2 3.2 %ends.1 = f32[8,256,256]{2,1,0:T(8,128)S(1)} custom-call(s32[1]{0:T(128)} %bitcast.2.inner, s32[1]{0:T(128)} %bitcast.outer, f32[5,256,256]{2,1,0:T(8,128)S(1)} %base_powers.1.refs_4_, f32[7,256,256]{2,1,0:T(8,128)S(1)} %high_powers.1.high), custom_call_target="tpu_custom_call" | custom-call | flops 1 | bytes 1 | tf_op jit(solution)/shard_map/join_3/ends/pallas_call | solution.py:33
  43.1 3.7 %collective-permute-start.5 = (f32[264,256]{1,0:T(8,128)S(1)}, f32[264,256]{1,0:T(8,128)S(1)}, u32[]{:S(2)}, u32[]{:S(2)}) collective-permute-start(f32[264,256]{1,0:T(8,128)S(1)} %total.9.own), channel_id=1, source_target_pairs={{0,1},{1,0},{2,3},{3,2},{4,5},{5,4},{6,7},{7,6},{8,9},{9,8},{10,11... | collective-permute-start | bytes 811016 | tf_op jit(solution)/shard_map/join_core/ppermute | solution.py:448
  48.3 1.7 %collective-permute-start.6 = (f32[264,256]{1,0:T(8,128)S(1)}, f32[264,256]{1,0:T(8,128)S(1)}, u32[]{:S(2)}, u32[]{:S(2)}) collective-permute-start(f32[264,256]{1,0:T(8,128)S(1)} %total.10.own), channel_id=1, source_target_pairs={{0,2},{1,3},{2,0},{3,1},{4,6},{5,7},{6,4},{7,5},{8,10},{9,11},{10,... | collective-permute-start | bytes 811016 | tf_op jit(solution)/shard_map/join_z/ppermute | solution.py:448
  50.1 2.2 %collective-permute-start.8 = (f32[264,256]{1,0:T(8,128)S(1)}, f32[264,256]{1,0:T(8,128)S(1)}, u32[]{:S(2)}, u32[]{:S(2)}) collective-permute-start(f32[264,256]{1,0:T(8,128)S(1)} %get-tuple-element.87.own), channel_id=1, source_target_pairs={{0,48},{16,32},{32,16},{48,0},{64,112},{80,96},{96,80},{112,64},{1... | collective-permute-start | bytes 811016 | tf_op jit(solution)/shard_map/join_3/ppermute | solution.py:448
  52.7 3.8 %collective-permute-done.6.other.chip_map = f32[264,256]{1,0:T(8,128)S(1)} collective-permute-done((f32[264,256]{1,0:T(8,128)S(1)}, f32[264,256]{1,0:T(8,128)S(1)}, u32[]{:S(2)}, u32[]{:S(2)}) %collective-permute-start.6) | collective-permute-done | bytes 270368 | tf_op jit(solution)/shard_map/join_z/ppermute | solution.py:448
  57.1 5.9 %collective-permute-start.7 = (f32[8,256]{1,0:T(8,128)S(1)}, f32[8,256]{1,0:T(8,128)S(1)}, u32[]{:S(2)}, u32[]{:S(2)}) collective-permute-start(f32[8,256]{1,0:T(8,128)S(1)} %hop.2), channel_id=1, source_target_pairs={{0,6},{1,7},{2,4},{3,5},{16,22},{17,23},{18,20},{19,21},{32,38},{3... | collective-permute-start | bytes 24584 | tf_op jit(solution)/shard_map/hop_0/ppermute | solution.py:537
  68.3 2.4 %collective-permute-done.11.other = f32[264,256]{1,0:T(8,128)S(1)} collective-permute-done((f32[264,256]{1,0:T(8,128)S(1)}, f32[264,256]{1,0:T(8,128)S(1)}, u32[]{:S(2)}, u32[]{:S(2)}) %collective-permute-start.11) | collective-permute-done | bytes 270368 | tf_op jit(solution)/shard_map/hop_0/ppermute | solution.py:448
  72.5 2.4 %collective-permute-start.13 = (f32[8,256]{1,0:T(8,128)S(1)}, f32[8,256]{1,0:T(8,128)S(1)}, u32[]{:S(2)}, u32[]{:S(2)}) collective-permute-start(f32[8,256]{1,0:T(8,128)S(1)} %get-tuple-element.104.own), channel_id=1, source_target_pairs={{0,192},{16,208},{32,224},{48,240},{64,128},{80,144},{96,160},{112... | collective-permute-start | bytes 24584 | tf_op jit(solution)/shard_map/spread_x/ppermute | solution.py:448
  76.5 3.6 %collective-permute-start.14 = (f32[8,256]{1,0:T(8,128)S(1)}, f32[8,256]{1,0:T(8,128)S(1)}, u32[]{:S(2)}, u32[]{:S(2)}) collective-permute-start(f32[8,256]{1,0:T(8,128)S(1)} %spread.4.own), channel_id=1, source_target_pairs={{0,1},{1,0},{2,3},{3,2},{4,5},{5,4},{6,7},{7,6},{8,9},{9,8},{10,11... | collective-permute-start | bytes 24584 | tf_op jit(solution)/shard_map/spread_core/ppermute | solution.py:448
  81.1 3.2 %states.1 = (f32[16,256]{1,0:T(8,128)S(1)}, f32[16,256]{1,0:T(8,128)}) custom-call(f32[8,256]{1,0:T(8,128)S(1)} %get-tuple-element.103.entry, f32[264,256]{1,0:T(8,128)S(1)} %get-tuple-element.110.before, f32[8,264,256]{2,1,0:T(8,128)S(1)} %get-tuple-element.111.even, f32[8,264,256]{2,1,0:T(8,128)S(1)} %get-tuple-element.112.odd, f32[16,256]{1,0:T(8,128)S(1)} %copy-done, ...), custom_call_target="tpu_custom_call" | custom-call | flops 1 | bytes 1 | tf_op jit(solution)/shard_map/spread_z0/states/pallas_call | solution.py:33
  84.5 3.8 %collective-permute-start.16 = (f32[8,256]{1,0:T(8,128)S(1)}, f32[8,256]{1,0:T(8,128)S(1)}, u32[]{:S(2)}, u32[]{:S(2)}) collective-permute-start(f32[8,256]{1,0:T(8,128)S(1)} %spread.6.own), channel_id=1, source_target_pairs={{0,4},{1,5},{2,6},{3,7},{4,0},{5,1},{6,2},{7,3},{8,12},{9,13},{10,... | collective-permute-start | bytes 24584 | tf_op jit(solution)/shard_map/spread_z1/ppermute | solution.py:448
  89.1 1.2 %local.1.base = f32[16,256]{1,0:T(8,128)S(1)} custom-call(f32[16,256]{1,0:T(8,128)S(1)} %get-tuple-element.117.pred, f32[16,256]{1,0:T(8,128)S(1)} %copy-done.1, f32[5,256,256]{2,1,0:T(8,128)S(1)} %base_powers.1.refs_4_), custom_call_target="tpu_custom_call" | custom-call | flops 1 | bytes 1 | tf_op jit(solution)/shard_map/spread_z1/local/pallas_call | solution.py:33
  91.1 5.1 %collective-permute-start.17 = (f32[8,256]{1,0:T(8,128)S(1)}, f32[8,256]{1,0:T(8,128)S(1)}, u32[]{:S(2)}, u32[]{:S(2)}) collective-permute-start(f32[8,256]{1,0:T(8,128)S(1)} %spread.7), channel_id=1, source_target_pairs={{0,14},{1,15},{2,12},{3,13},{4,10},{5,11},{6,8},{7,9},{8,6},{9,7},... | collective-permute-start | bytes 24584 | tf_op jit(solution)/shard_map/spread_z2/ppermute | solution.py:448
  97.2 2.3 %backward.1 = f32[16,256]{1,0:T(8,128)} custom-call(s32[1]{0:T(128)} %bitcast.2.inner, s32[1]{0:T(128)} %bitcast.outer, f32[8,256]{1,0:T(8,128)S(1)} %collective-permute-done.16.other.one, f32[8,256]{1,0:T(8,128)S(1)} %collective-permute-done.17.two, f32[8,256,256]{2,1,0:T(8,128)S(1)} %ends.1, f32[8,256]{1,0:T(8,128)S(1)} %gather.1.back, ...), custom_call_target="tpu_custom_call" | custom-call | flops 39321600 | bytes 1572864 | tf_op jit(solution)/shard_map/backward/backward/pallas_call | solution.py:33
  (53 shorter events, 19.5 us)
Async XLA Ops:
  0.6 0.7 copy-start
  1.4 0.7 copy-start.3
  2.0 11.4 %copy-start.4 = (f32[256,256]{1,0:T(8,128)S(1)}, f32[256,256]{1,0:T(8,128)}, u32[]{:S(2)}) copy-start(f32[256,256]{1,0:T(8,128)} %smooth.1) | copy-start | bytes 786436
  11.3 7.2 %collective-permute-start = (f32[264,256]{1,0:T(8,128)S(1)}, f32[264,256]{1,0:T(8,128)S(1)}, u32[]{:S(2)}, u32[]{:S(2)}) collective-permute-start(f32[264,256]{1,0:T(8,128)S(1)} %get-tuple-element.62.own.own_map), channel_id=1, source_target_pairs={{0,16},{16,0},{32,48},{48,32},{64,80},{80,64},{96,112},{112,96},{1... | collective-permute-start | bytes 811016 | tf_op jit(solution)/shard_map/join_0/ppermute | solution.py:403
  18.9 9.8 %collective-permute-start.1 = (f32[264,256]{1,0:T(8,128)S(1)}, f32[264,256]{1,0:T(8,128)S(1)}, u32[]{:S(2)}, u32[]{:S(2)}) collective-permute-start(f32[264,256]{1,0:T(8,128)S(1)} %total.6.own.own_map), channel_id=1, source_target_pairs={{0,48},{16,32},{32,16},{48,0},{64,112},{80,96},{96,80},{112,64},{1... | collective-permute-start | bytes 811016 | tf_op jit(solution)/shard_map/join_1/ppermute | solution.py:403
  29.1 6.6 %collective-permute-start.2 = (f32[264,256]{1,0:T(8,128)S(1)}, f32[264,256]{1,0:T(8,128)S(1)}, u32[]{:S(2)}, u32[]{:S(2)}) collective-permute-start(f32[264,256]{1,0:T(8,128)S(1)} %total.7.own.own_map), channel_id=1, source_target_pairs={{0,64},{16,80},{32,96},{48,112},{64,0},{80,16},{96,32},{112,48},{1... | collective-permute-start | bytes 811016 | tf_op jit(solution)/shard_map/join_2/ppermute | solution.py:448
  33.2 8.2 %collective-permute-start.4 = (f32[264,256]{1,0:T(8,128)S(1)}, f32[264,256]{1,0:T(8,128)S(1)}, u32[]{:S(2)}, u32[]{:S(2)}) collective-permute-start(f32[264,256]{1,0:T(8,128)S(1)} %offset_map.1.own), channel_id=1, source_target_pairs={{0,16},{16,0},{32,48},{48,32},{64,80},{80,64},{96,112},{112,96},{1... | collective-permute-start | bytes 811016 | tf_op jit(solution)/shard_map/join_2/ppermute | solution.py:448
  36.1 6.6 %collective-permute-start.3 = (f32[264,256]{1,0:T(8,128)S(1)}, f32[264,256]{1,0:T(8,128)S(1)}, u32[]{:S(2)}, u32[]{:S(2)}) collective-permute-start(f32[264,256]{1,0:T(8,128)S(1)} %total.8.own), channel_id=1, source_target_pairs={{0,192},{16,208},{32,224},{48,240},{64,128},{80,144},{96,160},{112... | collective-permute-start | bytes 811016 | tf_op jit(solution)/shard_map/join_3/ppermute | solution.py:448
  43.1 13.8 %copy-start.2 = (f32[256]{0:T(256)S(1)}, f32[256]{0:T(256)}, u32[]{:S(2)}) copy-start(f32[256]{0:T(256)} %param.9) | copy-start | bytes 3076
  43.1 4.8 %collective-permute-start.5 = (f32[264,256]{1,0:T(8,128)S(1)}, f32[264,256]{1,0:T(8,128)S(1)}, u32[]{:S(2)}, u32[]{:S(2)}) collective-permute-start(f32[264,256]{1,0:T(8,128)S(1)} %total.9.own), channel_id=1, source_target_pairs={{0,1},{1,0},{2,3},{3,2},{4,5},{5,4},{6,7},{7,6},{8,9},{9,8},{10,11... | collective-permute-start | bytes 811016 | tf_op jit(solution)/shard_map/join_core/ppermute | solution.py:448
  48.3 8.1 %collective-permute-start.6 = (f32[264,256]{1,0:T(8,128)S(1)}, f32[264,256]{1,0:T(8,128)S(1)}, u32[]{:S(2)}, u32[]{:S(2)}) collective-permute-start(f32[264,256]{1,0:T(8,128)S(1)} %total.10.own), channel_id=1, source_target_pairs={{0,2},{1,3},{2,0},{3,1},{4,6},{5,7},{6,4},{7,5},{8,10},{9,11},{10,... | collective-permute-start | bytes 811016 | tf_op jit(solution)/shard_map/join_z/ppermute | solution.py:448
  50.1 12.9 %collective-permute-start.8 = (f32[264,256]{1,0:T(8,128)S(1)}, f32[264,256]{1,0:T(8,128)S(1)}, u32[]{:S(2)}, u32[]{:S(2)}) collective-permute-start(f32[264,256]{1,0:T(8,128)S(1)} %get-tuple-element.87.own), channel_id=1, source_target_pairs={{0,48},{16,32},{32,16},{48,0},{64,112},{80,96},{96,80},{112,64},{1... | collective-permute-start | bytes 811016 | tf_op jit(solution)/shard_map/join_3/ppermute | solution.py:448
  57.1 7.0 %collective-permute-start.7 = (f32[8,256]{1,0:T(8,128)S(1)}, f32[8,256]{1,0:T(8,128)S(1)}, u32[]{:S(2)}, u32[]{:S(2)}) collective-permute-start(f32[8,256]{1,0:T(8,128)S(1)} %hop.2), channel_id=1, source_target_pairs={{0,6},{1,7},{2,4},{3,5},{16,22},{17,23},{18,20},{19,21},{32,38},{3... | collective-permute-start | bytes 24584 | tf_op jit(solution)/shard_map/hop_0/ppermute | solution.py:537
  64.1 6.6 %collective-permute-start.11 = (f32[264,256]{1,0:T(8,128)S(1)}, f32[264,256]{1,0:T(8,128)S(1)}, u32[]{:S(2)}, u32[]{:S(2)}) collective-permute-start(f32[264,256]{1,0:T(8,128)S(1)} %get-tuple-element.91.own), channel_id=1, source_target_pairs={{0,64},{16,80},{32,96},{48,112},{64,0},{80,16},{96,32},{112,48},{1... | collective-permute-start | bytes 811016 | tf_op jit(solution)/shard_map/hop_0/ppermute | solution.py:448
  64.4 7.3 %collective-permute-start.12 = (f32[264,256]{1,0:T(8,128)S(1)}, f32[264,256]{1,0:T(8,128)S(1)}, u32[]{:S(2)}, u32[]{:S(2)}) collective-permute-start(f32[264,256]{1,0:T(8,128)S(1)} %total.11.group_map), channel_id=1, source_target_pairs={{8,14},{9,15},{10,12},{11,13},{24,30},{25,31},{26,28},{27,29},{40,... | collective-permute-start | bytes 811016 | tf_op jit(solution)/shard_map/hop_1/ppermute | solution.py:547
  65.1 6.6 %collective-permute-start.10 = (f32[8,256]{1,0:T(8,128)S(1)}, f32[8,256]{1,0:T(8,128)S(1)}, u32[]{:S(2)}, u32[]{:S(2)}) collective-permute-start(f32[8,256]{1,0:T(8,128)S(1)} %hop.3), channel_id=1, source_target_pairs={{4,14},{5,15},{6,12},{7,13},{20,30},{21,31},{22,28},{23,29},{36,46... | collective-permute-start | bytes 24584 | tf_op jit(solution)/shard_map/hop_1/ppermute | solution.py:545
  65.8 6.0 %collective-permute-start.9 = (f32[8,256]{1,0:T(8,128)S(1)}, f32[8,256]{1,0:T(8,128)S(1)}, u32[]{:S(2)}, u32[]{:S(2)}) collective-permute-start(f32[8,256]{1,0:T(8,128)S(1)} %hop.3), channel_id=1, source_target_pairs={{4,10},{5,11},{6,8},{7,9},{20,26},{21,27},{22,24},{23,25},{36,42},... | collective-permute-start | bytes 24584 | tf_op jit(solution)/shard_map/hop_1/ppermute | solution.py:544
  72.5 3.7 %collective-permute-start.13 = (f32[8,256]{1,0:T(8,128)S(1)}, f32[8,256]{1,0:T(8,128)S(1)}, u32[]{:S(2)}, u32[]{:S(2)}) collective-permute-start(f32[8,256]{1,0:T(8,128)S(1)} %get-tuple-element.104.own), channel_id=1, source_target_pairs={{0,192},{16,208},{32,224},{48,240},{64,128},{80,144},{96,160},{112... | collective-permute-start | bytes 24584 | tf_op jit(solution)/shard_map/spread_x/ppermute | solution.py:448
  76.5 4.4 %collective-permute-start.14 = (f32[8,256]{1,0:T(8,128)S(1)}, f32[8,256]{1,0:T(8,128)S(1)}, u32[]{:S(2)}, u32[]{:S(2)}) collective-permute-start(f32[8,256]{1,0:T(8,128)S(1)} %spread.4.own), channel_id=1, source_target_pairs={{0,1},{1,0},{2,3},{3,2},{4,5},{5,4},{6,7},{7,6},{8,9},{9,8},{10,11... | collective-permute-start | bytes 24584 | tf_op jit(solution)/shard_map/spread_core/ppermute | solution.py:448
  81.1 3.2 %collective-permute-start.15 = (f32[8,256]{1,0:T(8,128)S(1)}, f32[8,256]{1,0:T(8,128)S(1)}, u32[]{:S(2)}, u32[]{:S(2)}) collective-permute-start(f32[8,256]{1,0:T(8,128)S(1)} %spread.5.own), channel_id=1, source_target_pairs={{0,2},{1,3},{2,0},{3,1},{4,6},{5,7},{6,4},{7,5},{8,10},{9,11},{10,... | collective-permute-start | bytes 24584 | tf_op jit(solution)/shard_map/spread_z0/ppermute | solution.py:448
  84.5 6.4 %collective-permute-start.16 = (f32[8,256]{1,0:T(8,128)S(1)}, f32[8,256]{1,0:T(8,128)S(1)}, u32[]{:S(2)}, u32[]{:S(2)}) collective-permute-start(f32[8,256]{1,0:T(8,128)S(1)} %spread.6.own), channel_id=1, source_target_pairs={{0,4},{1,5},{2,6},{3,7},{4,0},{5,1},{6,2},{7,3},{8,12},{9,13},{10,... | collective-permute-start | bytes 24584 | tf_op jit(solution)/shard_map/spread_z1/ppermute | solution.py:448
  88.3 0.7 copy-start.1
  91.1 6.1 %collective-permute-start.17 = (f32[8,256]{1,0:T(8,128)S(1)}, f32[8,256]{1,0:T(8,128)S(1)}, u32[]{:S(2)}, u32[]{:S(2)}) collective-permute-start(f32[8,256]{1,0:T(8,128)S(1)} %spread.7), channel_id=1, source_target_pairs={{0,14},{1,15},{2,12},{3,13},{4,10},{5,11},{6,8},{7,9},{8,6},{9,7},... | collective-permute-start | bytes 24584 | tf_op jit(solution)/shard_map/spread_z2/ppermute | solution.py:448

commit v3 on v1

--- a/solution.py
+++ b/solution.py
@@ -49,39 +49,65 @@
     for source, dest, k in small:
         pltpu.make_async_copy(source, dest, sems.at[k]).start()
     pairs = steps // 2
-    order = [2 * c + i for i in range(2) for c in range(pairs)]
-    for t in order:
+    for t in range(steps):
         pltpu.make_async_copy(jac_hbm.at[t], buf.at[t], sems.at[t]).start()
     for source, dest, k in small:
         pltpu.make_async_copy(source, dest, sems.at[k]).wait()
     g = gain[...]
     retain = 1.0 - g
-    for t in order:
-        pltpu.make_async_copy(jac_hbm.at[t], buf.at[t], sems.at[t]).wait()
-        c = t // 2
-        offset = jnp.broadcast_to(g * obs[t : t + 1, :], (PAD, n))
-        if t % 2 == 0:
-            chain[c, :n] = buf[t].T * retain
-            chain[c, n:] = offset
-        else:
-            moved = dot_nt(chain[c], buf[t]) * retain
-            chain[c, :n] = moved[:n]
-            chain[c, n:] = moved[n:] + offset
+
+    def offset(t):
+        return jnp.broadcast_to(g * obs[t : t + 1, :], (PAD, n))
+
+    def arrive(c):
+        for t in (2 * c, 2 * c + 1):
+            pltpu.make_async_copy(jac_hbm.at[t], buf.at[t], sems.at[t]).wait()
+
+    def begin(c):
+        chain[c, :n] = buf[2 * c].T * retain
+        chain[c, n:] = offset(2 * c)
+
+    def finish(c):
+        moved = dot_nt(chain[c], buf[2 * c + 1]) * retain
+        chain[c, :n] = moved[:n]
+        chain[c, n:] = moved[n:] + offset(2 * c + 1)
+
     kept = {(0, pairs): out, (0, pairs // 2): half}
     kept[(0, pairs // 4)] = quarter
     kept[(pairs // 2, 3 * pairs // 4)] = third
-    width = 1
-    while width < pairs:
-        for c in range(0, pairs, 2 * width):
-            moved = dot_nn(chain[c], chain[c + width, :n])
-            later = chain[c + width, n:]
-            span = (c, c + 2 * width)
-            dest = kept.get(span, chain.at[c])
-            dest[:n] = moved[:n]
-            dest[n:] = moved[n:] + later
-            if span in kept and 2 * width < pairs:
-                chain[c] = dest[...]
-        width *= 2
+
+    def merge(c, width):
+        moved = dot_nn(chain[c], chain[c + width, :n])
+        later = chain[c + width, n:]
+        span = (c, c + 2 * width)
+        dest = kept.get(span, chain.at[c])
+        dest[:n] = moved[:n]
+        dest[n:] = moved[n:] + later
+        if span in kept and 2 * width < pairs:
+            chain[c] = dest[...]
+
+    arrive(0)
+    begin(0)
+    waiting = []
+    for c in range(pairs):
+        if c + 1 < pairs:
+            arrive(c + 1)
+        ready, waiting = waiting, []
+        finish(c)
+        if c + 1 < pairs:
+            begin(c + 1)
+        for item in ready:
+            merge(*item)
+        if c % 2 == 1:
+            waiting.append((c - 1, 1))
+        for first, width in ready:
+            if (first // width) % 4 == 2 and 4 * width < pairs + 1:
+                waiting.append((first - 2 * width, 2 * width))
+    while waiting:
+        first, width = waiting.pop(0)
+        merge(first, width)
+        if (first // width) % 4 == 2 and 2 * width < pairs:
+            waiting.append((first - 2 * width, 2 * width))
 
 
 def local_map(place, jac, obs, gain):

time: 101 us -> 100 us (0.990)
  Pallas kernels: 44.8 us -> 43.7 us
    pallas_call x31, Pallas kernels: 44.8 us -> 43.7 us  [kernel_call(): pl.pallas_call(body, out_shape=shapes, in_specs=in_specs, out_specs=out_s...]
  transfers between devices with their start and end apart: 18 -> 18, of which waited for: 9 -> 9; matrix products, arithmetic and copies ran while one was open for 0% -> 0% of each run, Pallas kernels for 30% -> 31%
where the time goes in v3:
time: 100 us; the launch traced here: 98.5 us
  Pallas kernels  43.7 us (44%)
  starting transfers between devices  39.9 us (40%)
  waiting for transfers between devices  12.5 us (12%)
  local copies, waits for them, and re-layouts  1.4 us (1%)
    pallas_call x31, Pallas kernels, kernel_call(): pl.pallas_call(body, out_shape=shapes, in_specs=in_specs, out_specs=out_s...  43.7 us
    ppermute x12, starting transfers between devices, partner(): lax.ppermute(value, axis, [(i, i ^ flip) for i in range(counts[axis])])  25.6 us
    ppermute x12, waiting for transfers between devices, partner(): lax.ppermute(value, axis, [(i, i ^ flip) for i in range(counts[axis])])  12.3 us
    ppermute x2, starting transfers between devices, exchange(): lax.ppermute(total, axis, [(i, i ^ flip) for i in range(counts[axis])])  6.3 us
    ppermute x1, starting transfers between devices, shards(): arrived = lax.ppermute(y, 'outer', mirror(0, 1))  5.85 us
  transfers between devices with their start and end apart: 18, of which 9 were waited for; matrix products, arithmetic and copies ran while one was open for 0% of the time, Pallas kernels for 31%

profile of v3, /device:TPU:1, one launch (start us, length us, event | category | flops | bytes accessed | tf_op | source)
XLA Modules:
  0.0 98.5 jit_solution(13024432574767731189)
XLA Ops:
  2.0 8.1 %local_map.1 = (f32[264,256]{1,0:T(8,128)S(1)}, f32[264,256]{1,0:T(8,128)S(1)}, f32[264,256]{1,0:T(8,128)S(1)}, f32[264,256]{1,0:T(8,128)S(1)}, f32[16,256,256]{2,1,0:T(8,128)S(1)}) custom-call(s32[1]{0:T(128)} %bitcast.2.inner, s32[1]{0:T(128)} %bitcast.outer, f32[16,256,256]{2,1,0:T(8,128)} %jac_hbm.1, f32[16,256]{1,0:T(8,128)S(1)} %copy-done, ...), custom_call_target="tpu_custom_call" | custom-call | flops 3221225472 | bytes 4194304 | tf_op jit(solution)/shard_map/compose/local_map/pallas_call | solution.py:33
  10.1 2.2 %collective-permute-start = (f32[264,256]{1,0:T(8,128)S(1)}, f32[264,256]{1,0:T(8,128)S(1)}, u32[]{:S(2)}, u32[]{:S(2)}) collective-permute-start(f32[264,256]{1,0:T(8,128)S(1)} %get-tuple-element.78.own.own_map), channel_id=1, source_target_pairs={{0,16},{16,0},{32,48},{48,32},{64,80},{80,64},{96,112},{112,96},{1... | collective-permute-start | bytes 811016 | tf_op jit(solution)/shard_map/join_0/ppermute | solution.py:431
  12.4 4.8 %maps.2 = (f32[8,264,256]{2,1,0:T(8,128)S(1)}, f32[4,264,256]{2,1,0:T(8,128)S(1)}, f32[4,264,256]{2,1,0:T(8,128)S(1)}) custom-call(f32[264,256]{1,0:T(8,128)S(1)} %get-tuple-element.79.refs_0_, f32[264,256]{1,0:T(8,128)S(1)} %get-tuple-element.80.refs_1_, f32[264,256]{1,0:T(8,128)S(1)} %get-tuple-element.81.refs_2_, ...), custom_call_target="tpu_custom_call" | custom-call | flops 1610612736 | bytes 6291456 | tf_op jit(solution)/shard_map/join_0/maps/pallas_call | solution.py:33
  17.7 4.1 %collective-permute-start.1 = (f32[264,256]{1,0:T(8,128)S(1)}, f32[264,256]{1,0:T(8,128)S(1)}, u32[]{:S(2)}, u32[]{:S(2)}) collective-permute-start(f32[264,256]{1,0:T(8,128)S(1)} %total.6.own.own_map), channel_id=1, source_target_pairs={{0,48},{16,32},{32,16},{48,0},{64,112},{80,96},{96,80},{112,64},{1... | collective-permute-start | bytes 811016 | tf_op jit(solution)/shard_map/join_1/ppermute | solution.py:431
  21.8 1.7 %base_powers.1.refs_4_ = f32[5,256,256]{2,1,0:T(8,128)S(1)} custom-call(f32[256,256]{1,0:T(8,128)S(1)} %copy-done.4), custom_call_target="tpu_custom_call" | custom-call | flops 1006632960 | bytes 1572864 | tf_op jit(solution)/shard_map/join_1/base_powers/pallas_call | solution.py:33
  23.5 4.0 %maps.3 = (f32[8,264,256]{2,1,0:T(8,128)S(1)}, f32[4,264,256]{2,1,0:T(8,128)S(1)}) custom-call(f32[4,264,256]{2,1,0:T(8,128)S(1)} %get-tuple-element.87.refs_0_, f32[16,256,256]{2,1,0:T(8,128)S(1)} %get-tuple-element.82.refs_3_.refs_1_, f32[16,256]{1,0:T(8,128)S(1)} %copy-done, f32[1,256]{1,0:T(1,128)S(1)} %bitcast.10, f32[5,256,256]{2,1,0:T(8,128)S(1)} %base_powers.1.refs_4_), custom_call_target="tpu_custom_call" | custom-call | flops 1610612736 | bytes 6291456 | tf_op jit(solution)/shard_map/join_1/maps/pallas_call | solution.py:33
  27.9 1.3 %collective-permute-start.2 = (f32[264,256]{1,0:T(8,128)S(1)}, f32[264,256]{1,0:T(8,128)S(1)}, u32[]{:S(2)}, u32[]{:S(2)}) collective-permute-start(f32[264,256]{1,0:T(8,128)S(1)} %total.7.own.own_map), channel_id=1, source_target_pairs={{0,64},{16,80},{32,96},{48,112},{64,0},{80,16},{96,32},{112,48},{1... | collective-permute-start | bytes 811016 | tf_op jit(solution)/shard_map/join_2/ppermute | solution.py:476
  29.2 2.8 %offset_map.1.own = f32[264,256]{1,0:T(8,128)S(1)} custom-call(f32[4,264,256]{2,1,0:T(8,128)S(1)} %get-tuple-element.92.even, f32[4,264,256]{2,1,0:T(8,128)S(1)} %get-tuple-element.93.odd, f32[5,256,256]{2,1,0:T(8,128)S(1)} %base_powers.1.refs_4_), custom_call_target="tpu_custom_call" | custom-call | flops 1409286144 | bytes 2359296 | tf_op jit(solution)/shard_map/join_2/offset_map/pallas_call | solution.py:33
  32.2 2.4 %high_powers.1.high = f32[7,256,256]{2,1,0:T(8,128)S(1)} custom-call(f32[5,256,256]{2,1,0:T(8,128)S(1)} %base_powers.1.refs_4_), custom_call_target="tpu_custom_call" | custom-call | flops 1207959552 | bytes 1835008 | tf_op jit(solution)/shard_map/join_2/high_powers/pallas_call | solution.py:33
  35.0 2.2 %collective-permute-start.3 = (f32[264,256]{1,0:T(8,128)S(1)}, f32[264,256]{1,0:T(8,128)S(1)}, u32[]{:S(2)}, u32[]{:S(2)}) collective-permute-start(f32[264,256]{1,0:T(8,128)S(1)} %total.8.own), channel_id=1, source_target_pairs={{0,192},{16,208},{32,224},{48,240},{64,128},{80,144},{96,160},{112... | collective-permute-start | bytes 811016 | tf_op jit(solution)/shard_map/join_3/ppermute | solution.py:476
  39.1 2.5 %collective-permute-done.3.other.row_map = f32[264,256]{1,0:T(8,128)S(1)} collective-permute-done((f32[264,256]{1,0:T(8,128)S(1)}, f32[264,256]{1,0:T(8,128)S(1)}, u32[]{:S(2)}, u32[]{:S(2)}) %collective-permute-start.3) | collective-permute-done | bytes 270368 | tf_op jit(solution)/shard_map/join_3/ppermute | solution.py:476
  42.0 3.7 %collective-permute-start.5 = (f32[264,256]{1,0:T(8,128)S(1)}, f32[264,256]{1,0:T(8,128)S(1)}, u32[]{:S(2)}, u32[]{:S(2)}) collective-permute-start(f32[264,256]{1,0:T(8,128)S(1)} %total.9.own), channel_id=1, source_target_pairs={{0,1},{1,0},{2,3},{3,2},{4,5},{5,4},{6,7},{7,6},{8,9},{9,8},{10,11... | collective-permute-start | bytes 811016 | tf_op jit(solution)/shard_map/join_core/ppermute | solution.py:476
  47.2 1.7 %collective-permute-start.6 = (f32[264,256]{1,0:T(8,128)S(1)}, f32[264,256]{1,0:T(8,128)S(1)}, u32[]{:S(2)}, u32[]{:S(2)}) collective-permute-start(f32[264,256]{1,0:T(8,128)S(1)} %total.10.own), channel_id=1, source_target_pairs={{0,2},{1,3},{2,0},{3,1},{4,6},{5,7},{6,4},{7,5},{8,10},{9,11},{10,... | collective-permute-start | bytes 811016 | tf_op jit(solution)/shard_map/join_z/ppermute | solution.py:476
  49.0 2.2 %collective-permute-start.8 = (f32[264,256]{1,0:T(8,128)S(1)}, f32[264,256]{1,0:T(8,128)S(1)}, u32[]{:S(2)}, u32[]{:S(2)}) collective-permute-start(f32[264,256]{1,0:T(8,128)S(1)} %get-tuple-element.103.own), channel_id=1, source_target_pairs={{0,48},{16,32},{32,16},{48,0},{64,112},{80,96},{96,80},{112,64},{1... | collective-permute-start | bytes 811016 | tf_op jit(solution)/shard_map/join_3/ppermute | solution.py:476
  51.3 4.1 %collective-permute-done.6.other.chip_map = f32[264,256]{1,0:T(8,128)S(1)} collective-permute-done((f32[264,256]{1,0:T(8,128)S(1)}, f32[264,256]{1,0:T(8,128)S(1)}, u32[]{:S(2)}, u32[]{:S(2)}) %collective-permute-start.6) | collective-permute-done | bytes 270368 | tf_op jit(solution)/shard_map/join_z/ppermute | solution.py:476
  56.1 5.8 %collective-permute-start.7 = (f32[8,256]{1,0:T(8,128)S(1)}, f32[8,256]{1,0:T(8,128)S(1)}, u32[]{:S(2)}, u32[]{:S(2)}) collective-permute-start(f32[8,256]{1,0:T(8,128)S(1)} %hop.2), channel_id=1, source_target_pairs={{0,6},{1,7},{2,4},{3,5},{16,22},{17,23},{18,20},{19,21},{32,38},{3... | collective-permute-start | bytes 24584 | tf_op jit(solution)/shard_map/hop_0/ppermute | solution.py:556
  67.5 2.1 %collective-permute-done.11.other = f32[264,256]{1,0:T(8,128)S(1)} collective-permute-done((f32[264,256]{1,0:T(8,128)S(1)}, f32[264,256]{1,0:T(8,128)S(1)}, u32[]{:S(2)}, u32[]{:S(2)}) %collective-permute-start.11) | collective-permute-done | bytes 270368 | tf_op jit(solution)/shard_map/hop_0/ppermute | solution.py:476
  71.5 2.4 %collective-permute-start.13 = (f32[8,256]{1,0:T(8,128)S(1)}, f32[8,256]{1,0:T(8,128)S(1)}, u32[]{:S(2)}, u32[]{:S(2)}) collective-permute-start(f32[8,256]{1,0:T(8,128)S(1)} %get-tuple-element.122.own), channel_id=1, source_target_pairs={{0,192},{16,208},{32,224},{48,240},{64,128},{80,144},{96,160},{112... | collective-permute-start | bytes 24584 | tf_op jit(solution)/shard_map/spread_x/ppermute | solution.py:476
  75.4 3.6 %collective-permute-start.14 = (f32[8,256]{1,0:T(8,128)S(1)}, f32[8,256]{1,0:T(8,128)S(1)}, u32[]{:S(2)}, u32[]{:S(2)}) collective-permute-start(f32[8,256]{1,0:T(8,128)S(1)} %spread.4.own), channel_id=1, source_target_pairs={{0,1},{1,0},{2,3},{3,2},{4,5},{5,4},{6,7},{7,6},{8,9},{9,8},{10,11... | collective-permute-start | bytes 24584 | tf_op jit(solution)/shard_map/spread_core/ppermute | solution.py:476
  80.0 2.2 %ends.1 = (f32[256,256]{1,0:T(8,128)S(1)}, f32[256,256]{1,0:T(8,128)S(1)}, f32[256,256]{1,0:T(8,128)S(1)}, f32[256,256]{1,0:T(8,128)S(1)}, f32[256,256]{1,0:T(8,128)S(1)}) custom-call(s32[1]{0:T(128)} %bitcast.2.inner, s32[1]{0:T(128)} %bitcast.outer, f32[256,256]{1,0:T(8,128)S(1)} %get-tuple-element.135.lift, f32[5,256,256]{2,1,0:T(8,128)S(1)} %base_powers.1.refs_4_, ...), custom_call_target="tpu_custom_call" | custom-call | flops 1006632960 | bytes 2359296 | tf_op jit(solution)/shard_map/spread_z0/ends/pallas_call | solution.py:33
  82.7 3.9 %collective-permute-start.16 = (f32[8,256]{1,0:T(8,128)S(1)}, f32[8,256]{1,0:T(8,128)S(1)}, u32[]{:S(2)}, u32[]{:S(2)}) collective-permute-start(f32[8,256]{1,0:T(8,128)S(1)} %spread.6.own), channel_id=1, source_target_pairs={{0,4},{1,5},{2,6},{3,7},{4,0},{5,1},{6,2},{7,3},{8,12},{9,13},{10,... | collective-permute-start | bytes 24584 | tf_op jit(solution)/shard_map/spread_z1/ppermute | solution.py:476
  86.6 3.2 %states.1 = (f32[16,256]{1,0:T(8,128)S(1)}, f32[16,256]{1,0:T(8,128)}) custom-call(f32[8,256]{1,0:T(8,128)S(1)} %get-tuple-element.121.entry, f32[264,256]{1,0:T(8,128)S(1)} %get-tuple-element.130.before, f32[8,264,256]{2,1,0:T(8,128)S(1)} %get-tuple-element.131.even, f32[8,264,256]{2,1,0:T(8,128)S(1)} %get-tuple-element.132.odd, f32[16,256]{1,0:T(8,128)S(1)} %copy-done, ...), custom_call_target="tpu_custom_call" | custom-call | flops 106954752 | bytes 4456448 | tf_op jit(solution)/shard_map/spread_z1/states/pallas_call | solution.py:33
  90.1 4.4 %collective-permute-start.17 = (f32[8,256]{1,0:T(8,128)S(1)}, f32[8,256]{1,0:T(8,128)S(1)}, u32[]{:S(2)}, u32[]{:S(2)}) collective-permute-start(f32[8,256]{1,0:T(8,128)S(1)} %spread.7), channel_id=1, source_target_pairs={{0,14},{1,15},{2,12},{3,13},{4,10},{5,11},{6,8},{7,9},{8,6},{9,7},... | collective-permute-start | bytes 24584 | tf_op jit(solution)/shard_map/spread_z2/ppermute | solution.py:476
  96.5 2.0 %backward.1 = f32[16,256]{1,0:T(8,128)} custom-call(s32[1]{0:T(128)} %bitcast.2.inner, s32[1]{0:T(128)} %bitcast.outer, f32[8,256]{1,0:T(8,128)S(1)} %collective-permute-done.17.other, f32[256,256]{1,0:T(8,128)S(1)} %get-tuple-element.151.end, f32[8,256]{1,0:T(8,128)S(1)} %gather.1.back, f32[5,256,256]{2,1,0:T(8,128)S(1)} %base_powers.1.refs_4_, ...), custom_call_target="tpu_custom_call" | custom-call | flops 39321600 | bytes 1572864 | tf_op jit(solution)/shard_map/backward/backward/pallas_call | solution.py:33
  (53 shorter events, 20.1 us)
Async XLA Ops:
  0.6 0.7 copy-start
  1.4 0.7 copy-start.3
  2.0 10.3 %copy-start.4 = (f32[256,256]{1,0:T(8,128)S(1)}, f32[256,256]{1,0:T(8,128)}, u32[]{:S(2)}) copy-start(f32[256,256]{1,0:T(8,128)} %smooth.1) | copy-start | bytes 786436
  10.1 7.2 %collective-permute-start = (f32[264,256]{1,0:T(8,128)S(1)}, f32[264,256]{1,0:T(8,128)S(1)}, u32[]{:S(2)}, u32[]{:S(2)}) collective-permute-start(f32[264,256]{1,0:T(8,128)S(1)} %get-tuple-element.78.own.own_map), channel_id=1, source_target_pairs={{0,16},{16,0},{32,48},{48,32},{64,80},{80,64},{96,112},{112,96},{1... | collective-permute-start | bytes 811016 | tf_op jit(solution)/shard_map/join_0/ppermute | solution.py:431
  17.7 9.8 %collective-permute-start.1 = (f32[264,256]{1,0:T(8,128)S(1)}, f32[264,256]{1,0:T(8,128)S(1)}, u32[]{:S(2)}, u32[]{:S(2)}) collective-permute-start(f32[264,256]{1,0:T(8,128)S(1)} %total.6.own.own_map), channel_id=1, source_target_pairs={{0,48},{16,32},{32,16},{48,0},{64,112},{80,96},{96,80},{112,64},{1... | collective-permute-start | bytes 811016 | tf_op jit(solution)/shard_map/join_1/ppermute | solution.py:431
  27.9 6.6 %collective-permute-start.2 = (f32[264,256]{1,0:T(8,128)S(1)}, f32[264,256]{1,0:T(8,128)S(1)}, u32[]{:S(2)}, u32[]{:S(2)}) collective-permute-start(f32[264,256]{1,0:T(8,128)S(1)} %total.7.own.own_map), channel_id=1, source_target_pairs={{0,64},{16,80},{32,96},{48,112},{64,0},{80,16},{96,32},{112,48},{1... | collective-permute-start | bytes 811016 | tf_op jit(solution)/shard_map/join_2/ppermute | solution.py:476
  32.1 5.9 %collective-permute-start.4 = (f32[264,256]{1,0:T(8,128)S(1)}, f32[264,256]{1,0:T(8,128)S(1)}, u32[]{:S(2)}, u32[]{:S(2)}) collective-permute-start(f32[264,256]{1,0:T(8,128)S(1)} %offset_map.1.own), channel_id=1, source_target_pairs={{0,16},{16,0},{32,48},{48,32},{64,80},{80,64},{96,112},{112,96},{1... | collective-permute-start | bytes 811016 | tf_op jit(solution)/shard_map/join_2/ppermute | solution.py:476
  35.0 6.6 %collective-permute-start.3 = (f32[264,256]{1,0:T(8,128)S(1)}, f32[264,256]{1,0:T(8,128)S(1)}, u32[]{:S(2)}, u32[]{:S(2)}) collective-permute-start(f32[264,256]{1,0:T(8,128)S(1)} %total.8.own), channel_id=1, source_target_pairs={{0,192},{16,208},{32,224},{48,240},{64,128},{80,144},{96,160},{112... | collective-permute-start | bytes 811016 | tf_op jit(solution)/shard_map/join_3/ppermute | solution.py:476
  42.0 13.8 %copy-start.2 = (f32[256]{0:T(256)S(1)}, f32[256]{0:T(256)}, u32[]{:S(2)}) copy-start(f32[256]{0:T(256)} %param.9) | copy-start | bytes 3076
  42.0 4.8 %collective-permute-start.5 = (f32[264,256]{1,0:T(8,128)S(1)}, f32[264,256]{1,0:T(8,128)S(1)}, u32[]{:S(2)}, u32[]{:S(2)}) collective-permute-start(f32[264,256]{1,0:T(8,128)S(1)} %total.9.own), channel_id=1, source_target_pairs={{0,1},{1,0},{2,3},{3,2},{4,5},{5,4},{6,7},{7,6},{8,9},{9,8},{10,11... | collective-permute-start | bytes 811016 | tf_op jit(solution)/shard_map/join_core/ppermute | solution.py:476
  47.2 8.2 %collective-permute-start.6 = (f32[264,256]{1,0:T(8,128)S(1)}, f32[264,256]{1,0:T(8,128)S(1)}, u32[]{:S(2)}, u32[]{:S(2)}) collective-permute-start(f32[264,256]{1,0:T(8,128)S(1)} %total.10.own), channel_id=1, source_target_pairs={{0,2},{1,3},{2,0},{3,1},{4,6},{5,7},{6,4},{7,5},{8,10},{9,11},{10,... | collective-permute-start | bytes 811016 | tf_op jit(solution)/shard_map/join_z/ppermute | solution.py:476
  49.0 12.9 %collective-permute-start.8 = (f32[264,256]{1,0:T(8,128)S(1)}, f32[264,256]{1,0:T(8,128)S(1)}, u32[]{:S(2)}, u32[]{:S(2)}) collective-permute-start(f32[264,256]{1,0:T(8,128)S(1)} %get-tuple-element.103.own), channel_id=1, source_target_pairs={{0,48},{16,32},{32,16},{48,0},{64,112},{80,96},{96,80},{112,64},{1... | collective-permute-start | bytes 811016 | tf_op jit(solution)/shard_map/join_3/ppermute | solution.py:476
  56.1 7.0 %collective-permute-start.7 = (f32[8,256]{1,0:T(8,128)S(1)}, f32[8,256]{1,0:T(8,128)S(1)}, u32[]{:S(2)}, u32[]{:S(2)}) collective-permute-start(f32[8,256]{1,0:T(8,128)S(1)} %hop.2), channel_id=1, source_target_pairs={{0,6},{1,7},{2,4},{3,5},{16,22},{17,23},{18,20},{19,21},{32,38},{3... | collective-permute-start | bytes 24584 | tf_op jit(solution)/shard_map/hop_0/ppermute | solution.py:556
  63.0 6.6 %collective-permute-start.11 = (f32[264,256]{1,0:T(8,128)S(1)}, f32[264,256]{1,0:T(8,128)S(1)}, u32[]{:S(2)}, u32[]{:S(2)}) collective-permute-start(f32[264,256]{1,0:T(8,128)S(1)} %get-tuple-element.107.own), channel_id=1, source_target_pairs={{0,64},{16,80},{32,96},{48,112},{64,0},{80,16},{96,32},{112,48},{1... | collective-permute-start | bytes 811016 | tf_op jit(solution)/shard_map/hop_0/ppermute | solution.py:476
  63.3 7.3 %collective-permute-start.12 = (f32[264,256]{1,0:T(8,128)S(1)}, f32[264,256]{1,0:T(8,128)S(1)}, u32[]{:S(2)}, u32[]{:S(2)}) collective-permute-start(f32[264,256]{1,0:T(8,128)S(1)} %total.11.group_map), channel_id=1, source_target_pairs={{8,14},{9,15},{10,12},{11,13},{24,30},{25,31},{26,28},{27,29},{40,... | collective-permute-start | bytes 811016 | tf_op jit(solution)/shard_map/hop_1/ppermute | solution.py:566
  64.2 6.4 %collective-permute-start.10 = (f32[8,256]{1,0:T(8,128)S(1)}, f32[8,256]{1,0:T(8,128)S(1)}, u32[]{:S(2)}, u32[]{:S(2)}) collective-permute-start(f32[8,256]{1,0:T(8,128)S(1)} %hop.3), channel_id=1, source_target_pairs={{4,14},{5,15},{6,12},{7,13},{20,30},{21,31},{22,28},{23,29},{36,46... | collective-permute-start | bytes 24584 | tf_op jit(solution)/shard_map/hop_1/ppermute | solution.py:564
  64.9 5.8 %collective-permute-start.9 = (f32[8,256]{1,0:T(8,128)S(1)}, f32[8,256]{1,0:T(8,128)S(1)}, u32[]{:S(2)}, u32[]{:S(2)}) collective-permute-start(f32[8,256]{1,0:T(8,128)S(1)} %hop.3), channel_id=1, source_target_pairs={{4,10},{5,11},{6,8},{7,9},{20,26},{21,27},{22,24},{23,25},{36,42},... | collective-permute-start | bytes 24584 | tf_op jit(solution)/shard_map/hop_1/ppermute | solution.py:563
  71.5 3.7 %collective-permute-start.13 = (f32[8,256]{1,0:T(8,128)S(1)}, f32[8,256]{1,0:T(8,128)S(1)}, u32[]{:S(2)}, u32[]{:S(2)}) collective-permute-start(f32[8,256]{1,0:T(8,128)S(1)} %get-tuple-element.122.own), channel_id=1, source_target_pairs={{0,192},{16,208},{32,224},{48,240},{64,128},{80,144},{96,160},{112... | collective-permute-start | bytes 24584 | tf_op jit(solution)/shard_map/spread_x/ppermute | solution.py:476
  75.4 4.4 %collective-permute-start.14 = (f32[8,256]{1,0:T(8,128)S(1)}, f32[8,256]{1,0:T(8,128)S(1)}, u32[]{:S(2)}, u32[]{:S(2)}) collective-permute-start(f32[8,256]{1,0:T(8,128)S(1)} %spread.4.own), channel_id=1, source_target_pairs={{0,1},{1,0},{2,3},{3,2},{4,5},{5,4},{6,7},{7,6},{8,9},{9,8},{10,11... | collective-permute-start | bytes 24584 | tf_op jit(solution)/shard_map/spread_core/ppermute | solution.py:476
  80.0 2.5 %collective-permute-start.15 = (f32[8,256]{1,0:T(8,128)S(1)}, f32[8,256]{1,0:T(8,128)S(1)}, u32[]{:S(2)}, u32[]{:S(2)}) collective-permute-start(f32[8,256]{1,0:T(8,128)S(1)} %spread.5.own), channel_id=1, source_target_pairs={{0,2},{1,3},{2,0},{3,1},{4,6},{5,7},{6,4},{7,5},{8,10},{9,11},{10,... | collective-permute-start | bytes 24584 | tf_op jit(solution)/shard_map/spread_z0/ppermute | solution.py:476
  82.7 7.1 %collective-permute-start.16 = (f32[8,256]{1,0:T(8,128)S(1)}, f32[8,256]{1,0:T(8,128)S(1)}, u32[]{:S(2)}, u32[]{:S(2)}) collective-permute-start(f32[8,256]{1,0:T(8,128)S(1)} %spread.6.own), channel_id=1, source_target_pairs={{0,4},{1,5},{2,6},{3,7},{4,0},{5,1},{6,2},{7,3},{8,12},{9,13},{10,... | collective-permute-start | bytes 24584 | tf_op jit(solution)/shard_map/spread_z1/ppermute | solution.py:476
  89.9 5.4 %copy-start.1 = (f32[16,256]{1,0:T(8,128)S(1)}, f32[16,256]{1,0:T(8,128)}, u32[]{:S(2)}) copy-start(f32[16,256]{1,0:T(8,128)} %get-tuple-element.76.filt) | copy-start | bytes 49156
  90.1 6.4 %collective-permute-start.17 = (f32[8,256]{1,0:T(8,128)S(1)}, f32[8,256]{1,0:T(8,128)S(1)}, u32[]{:S(2)}, u32[]{:S(2)}) collective-permute-start(f32[8,256]{1,0:T(8,128)S(1)} %spread.7), channel_id=1, source_target_pairs={{0,14},{1,15},{2,12},{3,13},{4,10},{5,11},{6,8},{7,9},{8,6},{9,7},... | collective-permute-start | bytes 24584 | tf_op jit(solution)/shard_map/spread_z2/ppermute | solution.py:476

commit v4 on v3

--- a/solution.py
+++ b/solution.py
@@ -551,19 +551,22 @@
             for c in range(2)
         ]
 
+    def ahead(source, dest):
+        return [(source * group + k, dest * group + k) for k in range(group)]
+
     with jax.named_scope("hop_0"):
         y = hop(0, place, first, first, total)
-        arrived = lax.ppermute(y, "outer", mirror(0, 1))
+        arrived = lax.ppermute(y, "outer", ahead(0, 1))
         far, _ = lax.optimization_barrier((far, y))
         through, offsets = offsets_join(1, own_maps[1], other_maps[1], offsets, far)
         far = partner(offsets, "inner", 4)
         arrived, through = lax.optimization_barrier((arrived, through))
     with jax.named_scope("hop_1"):
         y = hop(1, place, first, arrived, total)
-        near = lax.ppermute(y, "outer", mirror(1, 2))
+        near = lax.ppermute(y, "outer", ahead(1, 2))
         farther = lax.ppermute(y, "outer", mirror(1, 3))
         sent_map, _ = lax.optimization_barrier((total, y))
-        skipped = lax.ppermute(sent_map, "outer", mirror(2, 3))
+        skipped = lax.ppermute(sent_map, "outer", ahead(2, 3))
         entry_map = kernel_call(
             entry_map_body,
             (n + PAD, n),
@@ -639,7 +642,7 @@
         others.append(other)
         value = spread(6, value, other)
     with jax.named_scope("spread_z2"):
-        other = partner(value, "outer", 14)
+        other = partner(value, "outer", 12)
         base = kernel_call(
             local_body,
             (steps, n),

time: 100 us -> 101 us (1.010)
  starting transfers between devices: 39.9 us -> 41.3 us
    ppermute x12, starting transfers between devices: 25.6 us -> 27.9 us  [partner(): lax.ppermute(value, axis, [(i, i ^ flip) for i in range(counts[axis])])]
  transfers between devices with their start and end apart: 18 -> 18, of which waited for: 9 -> 8; matrix products, arithmetic and copies ran while one was open for 0% -> 0% of each run, Pallas kernels for 31% -> 30%
where the time goes in v4:
time: 101 us; the launch traced here: 99.8 us
  Pallas kernels  43.7 us (43%)
  starting transfers between devices  41.3 us (41%)
  waiting for transfers between devices  12.4 us (12%)
  local copies, waits for them, and re-layouts  1.4 us (1%)
    pallas_call x31, Pallas kernels, kernel_call(): pl.pallas_call(body, out_shape=shapes, in_specs=in_specs, out_specs=out_s...  43.7 us
    ppermute x12, starting transfers between devices, partner(): lax.ppermute(value, axis, [(i, i ^ flip) for i in range(counts[axis])])  27.9 us
    ppermute x12, waiting for transfers between devices, partner(): lax.ppermute(value, axis, [(i, i ^ flip) for i in range(counts[axis])])  12.2 us
    ppermute x2, starting transfers between devices, exchange(): lax.ppermute(total, axis, [(i, i ^ flip) for i in range(counts[axis])])  6.3 us
    ppermute x1, starting transfers between devices, shards(): arrived = lax.ppermute(y, 'outer', ahead(0, 1))  4.87 us
  transfers between devices with their start and end apart: 18, of which 8 were waited for; matrix products, arithmetic and copies ran while one was open for 0% of the time, Pallas kernels for 30%

profile of v4, /device:TPU:1, one launch (start us, length us, event | category | flops | bytes accessed | tf_op | source)
XLA Modules:
  0.0 99.8 jit_solution(12336516120697644167)
XLA Ops:
  2.0 8.1 %local_map.1 = (f32[264,256]{1,0:T(8,128)S(1)}, f32[264,256]{1,0:T(8,128)S(1)}, f32[264,256]{1,0:T(8,128)S(1)}, f32[264,256]{1,0:T(8,128)S(1)}, f32[16,256,256]{2,1,0:T(8,128)S(1)}) custom-call(s32[1]{0:T(128)} %bitcast.2.inner, s32[1]{0:T(128)} %bitcast.outer, f32[16,256,256]{2,1,0:T(8,128)} %jac_hbm.1, f32[16,256]{1,0:T(8,128)S(1)} %copy-done, ...), custom_call_target="tpu_custom_call" | custom-call | flops 3221225472 | bytes 4194304 | tf_op jit(solution)/shard_map/compose/local_map/pallas_call | solution.py:33
  10.1 2.2 %collective-permute-start = (f32[264,256]{1,0:T(8,128)S(1)}, f32[264,256]{1,0:T(8,128)S(1)}, u32[]{:S(2)}, u32[]{:S(2)}) collective-permute-start(f32[264,256]{1,0:T(8,128)S(1)} %get-tuple-element.78.own.own_map), channel_id=1, source_target_pairs={{0,16},{16,0},{32,48},{48,32},{64,80},{80,64},{96,112},{112,96},{1... | collective-permute-start | bytes 811016 | tf_op jit(solution)/shard_map/join_0/ppermute | solution.py:431
  12.4 4.8 %maps.2 = (f32[8,264,256]{2,1,0:T(8,128)S(1)}, f32[4,264,256]{2,1,0:T(8,128)S(1)}, f32[4,264,256]{2,1,0:T(8,128)S(1)}) custom-call(f32[264,256]{1,0:T(8,128)S(1)} %get-tuple-element.79.refs_0_, f32[264,256]{1,0:T(8,128)S(1)} %get-tuple-element.80.refs_1_, f32[264,256]{1,0:T(8,128)S(1)} %get-tuple-element.81.refs_2_, ...), custom_call_target="tpu_custom_call" | custom-call | flops 1610612736 | bytes 6291456 | tf_op jit(solution)/shard_map/join_0/maps/pallas_call | solution.py:33
  17.7 4.1 %collective-permute-start.1 = (f32[264,256]{1,0:T(8,128)S(1)}, f32[264,256]{1,0:T(8,128)S(1)}, u32[]{:S(2)}, u32[]{:S(2)}) collective-permute-start(f32[264,256]{1,0:T(8,128)S(1)} %total.6.own.own_map), channel_id=1, source_target_pairs={{0,48},{16,32},{32,16},{48,0},{64,112},{80,96},{96,80},{112,64},{1... | collective-permute-start | bytes 811016 | tf_op jit(solution)/shard_map/join_1/ppermute | solution.py:431
  21.8 1.7 %base_powers.1.refs_4_ = f32[5,256,256]{2,1,0:T(8,128)S(1)} custom-call(f32[256,256]{1,0:T(8,128)S(1)} %copy-done.4), custom_call_target="tpu_custom_call" | custom-call | flops 1006632960 | bytes 1572864 | tf_op jit(solution)/shard_map/join_1/base_powers/pallas_call | solution.py:33
  23.5 4.0 %maps.3 = (f32[8,264,256]{2,1,0:T(8,128)S(1)}, f32[4,264,256]{2,1,0:T(8,128)S(1)}) custom-call(f32[4,264,256]{2,1,0:T(8,128)S(1)} %get-tuple-element.87.refs_0_, f32[16,256,256]{2,1,0:T(8,128)S(1)} %get-tuple-element.82.refs_3_.refs_1_, f32[16,256]{1,0:T(8,128)S(1)} %copy-done, f32[1,256]{1,0:T(1,128)S(1)} %bitcast.10, f32[5,256,256]{2,1,0:T(8,128)S(1)} %base_powers.1.refs_4_), custom_call_target="tpu_custom_call" | custom-call | flops 1610612736 | bytes 6291456 | tf_op jit(solution)/shard_map/join_1/maps/pallas_call | solution.py:33
  27.9 1.3 %collective-permute-start.2 = (f32[264,256]{1,0:T(8,128)S(1)}, f32[264,256]{1,0:T(8,128)S(1)}, u32[]{:S(2)}, u32[]{:S(2)}) collective-permute-start(f32[264,256]{1,0:T(8,128)S(1)} %total.7.own.own_map), channel_id=1, source_target_pairs={{0,64},{16,80},{32,96},{48,112},{64,0},{80,16},{96,32},{112,48},{1... | collective-permute-start | bytes 811016 | tf_op jit(solution)/shard_map/join_2/ppermute | solution.py:476
  29.2 2.8 %offset_map.1.own = f32[264,256]{1,0:T(8,128)S(1)} custom-call(f32[4,264,256]{2,1,0:T(8,128)S(1)} %get-tuple-element.92.even, f32[4,264,256]{2,1,0:T(8,128)S(1)} %get-tuple-element.93.odd, f32[5,256,256]{2,1,0:T(8,128)S(1)} %base_powers.1.refs_4_), custom_call_target="tpu_custom_call" | custom-call | flops 1409286144 | bytes 2359296 | tf_op jit(solution)/shard_map/join_2/offset_map/pallas_call | solution.py:33
  32.2 2.4 %high_powers.1.high = f32[7,256,256]{2,1,0:T(8,128)S(1)} custom-call(f32[5,256,256]{2,1,0:T(8,128)S(1)} %base_powers.1.refs_4_), custom_call_target="tpu_custom_call" | custom-call | flops 1207959552 | bytes 1835008 | tf_op jit(solution)/shard_map/join_2/high_powers/pallas_call | solution.py:33
  35.0 2.2 %collective-permute-start.3 = (f32[264,256]{1,0:T(8,128)S(1)}, f32[264,256]{1,0:T(8,128)S(1)}, u32[]{:S(2)}, u32[]{:S(2)}) collective-permute-start(f32[264,256]{1,0:T(8,128)S(1)} %total.8.own), channel_id=1, source_target_pairs={{0,192},{16,208},{32,224},{48,240},{64,128},{80,144},{96,160},{112... | collective-permute-start | bytes 811016 | tf_op jit(solution)/shard_map/join_3/ppermute | solution.py:476
  39.1 2.5 %collective-permute-done.3.other.row_map = f32[264,256]{1,0:T(8,128)S(1)} collective-permute-done((f32[264,256]{1,0:T(8,128)S(1)}, f32[264,256]{1,0:T(8,128)S(1)}, u32[]{:S(2)}, u32[]{:S(2)}) %collective-permute-start.3) | collective-permute-done | bytes 270368 | tf_op jit(solution)/shard_map/join_3/ppermute | solution.py:476
  42.0 3.7 %collective-permute-start.5 = (f32[264,256]{1,0:T(8,128)S(1)}, f32[264,256]{1,0:T(8,128)S(1)}, u32[]{:S(2)}, u32[]{:S(2)}) collective-permute-start(f32[264,256]{1,0:T(8,128)S(1)} %total.9.own), channel_id=1, source_target_pairs={{0,1},{1,0},{2,3},{3,2},{4,5},{5,4},{6,7},{7,6},{8,9},{9,8},{10,11... | collective-permute-start | bytes 811016 | tf_op jit(solution)/shard_map/join_core/ppermute | solution.py:476
  47.2 1.7 %collective-permute-start.6 = (f32[264,256]{1,0:T(8,128)S(1)}, f32[264,256]{1,0:T(8,128)S(1)}, u32[]{:S(2)}, u32[]{:S(2)}) collective-permute-start(f32[264,256]{1,0:T(8,128)S(1)} %total.10.own), channel_id=1, source_target_pairs={{0,2},{1,3},{2,0},{3,1},{4,6},{5,7},{6,4},{7,5},{8,10},{9,11},{10,... | collective-permute-start | bytes 811016 | tf_op jit(solution)/shard_map/join_z/ppermute | solution.py:476
  49.0 2.2 %collective-permute-start.8 = (f32[264,256]{1,0:T(8,128)S(1)}, f32[264,256]{1,0:T(8,128)S(1)}, u32[]{:S(2)}, u32[]{:S(2)}) collective-permute-start(f32[264,256]{1,0:T(8,128)S(1)} %get-tuple-element.103.own), channel_id=1, source_target_pairs={{0,48},{16,32},{32,16},{48,0},{64,112},{80,96},{96,80},{112,64},{1... | collective-permute-start | bytes 811016 | tf_op jit(solution)/shard_map/join_3/ppermute | solution.py:476
  51.3 4.1 %collective-permute-done.6.other.chip_map = f32[264,256]{1,0:T(8,128)S(1)} collective-permute-done((f32[264,256]{1,0:T(8,128)S(1)}, f32[264,256]{1,0:T(8,128)S(1)}, u32[]{:S(2)}, u32[]{:S(2)}) %collective-permute-start.6) | collective-permute-done | bytes 270368 | tf_op jit(solution)/shard_map/join_z/ppermute | solution.py:476
  56.1 4.9 %collective-permute-start.7 = (f32[8,256]{1,0:T(8,128)S(1)}, f32[8,256]{1,0:T(8,128)S(1)}, u32[]{:S(2)}, u32[]{:S(2)}) collective-permute-start(f32[8,256]{1,0:T(8,128)S(1)} %hop.2), channel_id=1, source_target_pairs={{0,4},{1,5},{2,6},{3,7},{16,20},{17,21},{18,22},{19,23},{32,36},{3... | collective-permute-start | bytes 24584 | tf_op jit(solution)/shard_map/hop_0/ppermute | solution.py:559
  66.5 2.3 %collective-permute-done.11.other = f32[264,256]{1,0:T(8,128)S(1)} collective-permute-done((f32[264,256]{1,0:T(8,128)S(1)}, f32[264,256]{1,0:T(8,128)S(1)}, u32[]{:S(2)}, u32[]{:S(2)}) %collective-permute-start.11) | collective-permute-done | bytes 270368 | tf_op jit(solution)/shard_map/hop_0/ppermute | solution.py:476
  70.7 2.4 %collective-permute-start.13 = (f32[8,256]{1,0:T(8,128)S(1)}, f32[8,256]{1,0:T(8,128)S(1)}, u32[]{:S(2)}, u32[]{:S(2)}) collective-permute-start(f32[8,256]{1,0:T(8,128)S(1)} %get-tuple-element.122.own), channel_id=1, source_target_pairs={{0,192},{16,208},{32,224},{48,240},{64,128},{80,144},{96,160},{112... | collective-permute-start | bytes 24584 | tf_op jit(solution)/shard_map/spread_x/ppermute | solution.py:476
  74.6 3.4 %collective-permute-start.14 = (f32[8,256]{1,0:T(8,128)S(1)}, f32[8,256]{1,0:T(8,128)S(1)}, u32[]{:S(2)}, u32[]{:S(2)}) collective-permute-start(f32[8,256]{1,0:T(8,128)S(1)} %spread.4.own), channel_id=1, source_target_pairs={{0,1},{1,0},{2,3},{3,2},{4,5},{5,4},{6,7},{7,6},{8,9},{9,8},{10,11... | collective-permute-start | bytes 24584 | tf_op jit(solution)/shard_map/spread_core/ppermute | solution.py:476
  80.3 2.2 %ends.1 = (f32[256,256]{1,0:T(8,128)S(1)}, f32[256,256]{1,0:T(8,128)S(1)}, f32[256,256]{1,0:T(8,128)S(1)}, f32[256,256]{1,0:T(8,128)S(1)}, f32[256,256]{1,0:T(8,128)S(1)}) custom-call(s32[1]{0:T(128)} %bitcast.2.inner, s32[1]{0:T(128)} %bitcast.outer, f32[256,256]{1,0:T(8,128)S(1)} %get-tuple-element.135.lift, f32[5,256,256]{2,1,0:T(8,128)S(1)} %base_powers.1.refs_4_, ...), custom_call_target="tpu_custom_call" | custom-call | flops 1006632960 | bytes 2359296 | tf_op jit(solution)/shard_map/spread_z0/ends/pallas_call | solution.py:33
  82.8 3.9 %collective-permute-start.16 = (f32[8,256]{1,0:T(8,128)S(1)}, f32[8,256]{1,0:T(8,128)S(1)}, u32[]{:S(2)}, u32[]{:S(2)}) collective-permute-start(f32[8,256]{1,0:T(8,128)S(1)} %spread.6.own), channel_id=1, source_target_pairs={{0,4},{1,5},{2,6},{3,7},{4,0},{5,1},{6,2},{7,3},{8,12},{9,13},{10,... | collective-permute-start | bytes 24584 | tf_op jit(solution)/shard_map/spread_z1/ppermute | solution.py:476
  86.6 3.2 %states.1 = (f32[16,256]{1,0:T(8,128)S(1)}, f32[16,256]{1,0:T(8,128)}) custom-call(f32[8,256]{1,0:T(8,128)S(1)} %get-tuple-element.121.entry, f32[264,256]{1,0:T(8,128)S(1)} %get-tuple-element.130.before, f32[8,264,256]{2,1,0:T(8,128)S(1)} %get-tuple-element.131.even, f32[8,264,256]{2,1,0:T(8,128)S(1)} %get-tuple-element.132.odd, f32[16,256]{1,0:T(8,128)S(1)} %copy-done, ...), custom_call_target="tpu_custom_call" | custom-call | flops 106954752 | bytes 4456448 | tf_op jit(solution)/shard_map/spread_z1/states/pallas_call | solution.py:33
  90.1 5.7 %collective-permute-start.17 = (f32[8,256]{1,0:T(8,128)S(1)}, f32[8,256]{1,0:T(8,128)S(1)}, u32[]{:S(2)}, u32[]{:S(2)}) collective-permute-start(f32[8,256]{1,0:T(8,128)S(1)} %spread.7), channel_id=1, source_target_pairs={{0,12},{1,13},{2,14},{3,15},{4,8},{5,9},{6,10},{7,11},{8,4},{9,5},... | collective-permute-start | bytes 24584 | tf_op jit(solution)/shard_map/spread_z2/ppermute | solution.py:476
  97.8 2.0 %backward.1 = f32[16,256]{1,0:T(8,128)} custom-call(s32[1]{0:T(128)} %bitcast.2.inner, s32[1]{0:T(128)} %bitcast.outer, f32[8,256]{1,0:T(8,128)S(1)} %collective-permute-done.17.other, f32[256,256]{1,0:T(8,128)S(1)} %get-tuple-element.151.end, f32[8,256]{1,0:T(8,128)S(1)} %gather.1.back, f32[5,256,256]{2,1,0:T(8,128)S(1)} %base_powers.1.refs_4_, ...), custom_call_target="tpu_custom_call" | custom-call | flops 39321600 | bytes 1572864 | tf_op jit(solution)/shard_map/backward/backward/pallas_call | solution.py:33
  (53 shorter events, 21.1 us)
Async XLA Ops:
  0.6 0.7 copy-start
  1.4 0.7 copy-start.3
  2.0 10.3 %copy-start.4 = (f32[256,256]{1,0:T(8,128)S(1)}, f32[256,256]{1,0:T(8,128)}, u32[]{:S(2)}) copy-start(f32[256,256]{1,0:T(8,128)} %smooth.1) | copy-start | bytes 786436
  10.1 7.2 %collective-permute-start = (f32[264,256]{1,0:T(8,128)S(1)}, f32[264,256]{1,0:T(8,128)S(1)}, u32[]{:S(2)}, u32[]{:S(2)}) collective-permute-start(f32[264,256]{1,0:T(8,128)S(1)} %get-tuple-element.78.own.own_map), channel_id=1, source_target_pairs={{0,16},{16,0},{32,48},{48,32},{64,80},{80,64},{96,112},{112,96},{1... | collective-permute-start | bytes 811016 | tf_op jit(solution)/shard_map/join_0/ppermute | solution.py:431
  17.7 9.8 %collective-permute-start.1 = (f32[264,256]{1,0:T(8,128)S(1)}, f32[264,256]{1,0:T(8,128)S(1)}, u32[]{:S(2)}, u32[]{:S(2)}) collective-permute-start(f32[264,256]{1,0:T(8,128)S(1)} %total.6.own.own_map), channel_id=1, source_target_pairs={{0,48},{16,32},{32,16},{48,0},{64,112},{80,96},{96,80},{112,64},{1... | collective-permute-start | bytes 811016 | tf_op jit(solution)/shard_map/join_1/ppermute | solution.py:431
  27.9 6.6 %collective-permute-start.2 = (f32[264,256]{1,0:T(8,128)S(1)}, f32[264,256]{1,0:T(8,128)S(1)}, u32[]{:S(2)}, u32[]{:S(2)}) collective-permute-start(f32[264,256]{1,0:T(8,128)S(1)} %total.7.own.own_map), channel_id=1, source_target_pairs={{0,64},{16,80},{32,96},{48,112},{64,0},{80,16},{96,32},{112,48},{1... | collective-permute-start | bytes 811016 | tf_op jit(solution)/shard_map/join_2/ppermute | solution.py:476
  32.1 5.9 %collective-permute-start.4 = (f32[264,256]{1,0:T(8,128)S(1)}, f32[264,256]{1,0:T(8,128)S(1)}, u32[]{:S(2)}, u32[]{:S(2)}) collective-permute-start(f32[264,256]{1,0:T(8,128)S(1)} %offset_map.1.own), channel_id=1, source_target_pairs={{0,16},{16,0},{32,48},{48,32},{64,80},{80,64},{96,112},{112,96},{1... | collective-permute-start | bytes 811016 | tf_op jit(solution)/shard_map/join_2/ppermute | solution.py:476
  35.0 6.6 %collective-permute-start.3 = (f32[264,256]{1,0:T(8,128)S(1)}, f32[264,256]{1,0:T(8,128)S(1)}, u32[]{:S(2)}, u32[]{:S(2)}) collective-permute-start(f32[264,256]{1,0:T(8,128)S(1)} %total.8.own), channel_id=1, source_target_pairs={{0,192},{16,208},{32,224},{48,240},{64,128},{80,144},{96,160},{112... | collective-permute-start | bytes 811016 | tf_op jit(solution)/shard_map/join_3/ppermute | solution.py:476
  42.0 13.8 %copy-start.2 = (f32[256]{0:T(256)S(1)}, f32[256]{0:T(256)}, u32[]{:S(2)}) copy-start(f32[256]{0:T(256)} %param.9) | copy-start | bytes 3076
  42.0 4.8 %collective-permute-start.5 = (f32[264,256]{1,0:T(8,128)S(1)}, f32[264,256]{1,0:T(8,128)S(1)}, u32[]{:S(2)}, u32[]{:S(2)}) collective-permute-start(f32[264,256]{1,0:T(8,128)S(1)} %total.9.own), channel_id=1, source_target_pairs={{0,1},{1,0},{2,3},{3,2},{4,5},{5,4},{6,7},{7,6},{8,9},{9,8},{10,11... | collective-permute-start | bytes 811016 | tf_op jit(solution)/shard_map/join_core/ppermute | solution.py:476
  47.2 8.2 %collective-permute-start.6 = (f32[264,256]{1,0:T(8,128)S(1)}, f32[264,256]{1,0:T(8,128)S(1)}, u32[]{:S(2)}, u32[]{:S(2)}) collective-permute-start(f32[264,256]{1,0:T(8,128)S(1)} %total.10.own), channel_id=1, source_target_pairs={{0,2},{1,3},{2,0},{3,1},{4,6},{5,7},{6,4},{7,5},{8,10},{9,11},{10,... | collective-permute-start | bytes 811016 | tf_op jit(solution)/shard_map/join_z/ppermute | solution.py:476
  49.0 12.0 %collective-permute-start.8 = (f32[264,256]{1,0:T(8,128)S(1)}, f32[264,256]{1,0:T(8,128)S(1)}, u32[]{:S(2)}, u32[]{:S(2)}) collective-permute-start(f32[264,256]{1,0:T(8,128)S(1)} %get-tuple-element.103.own), channel_id=1, source_target_pairs={{0,48},{16,32},{32,16},{48,0},{64,112},{80,96},{96,80},{112,64},{1... | collective-permute-start | bytes 811016 | tf_op jit(solution)/shard_map/join_3/ppermute | solution.py:476
  56.1 6.1 %collective-permute-start.7 = (f32[8,256]{1,0:T(8,128)S(1)}, f32[8,256]{1,0:T(8,128)S(1)}, u32[]{:S(2)}, u32[]{:S(2)}) collective-permute-start(f32[8,256]{1,0:T(8,128)S(1)} %hop.2), channel_id=1, source_target_pairs={{0,4},{1,5},{2,6},{3,7},{16,20},{17,21},{18,22},{19,23},{32,36},{3... | collective-permute-start | bytes 24584 | tf_op jit(solution)/shard_map/hop_0/ppermute | solution.py:559
  62.0 6.8 %collective-permute-start.11 = (f32[264,256]{1,0:T(8,128)S(1)}, f32[264,256]{1,0:T(8,128)S(1)}, u32[]{:S(2)}, u32[]{:S(2)}) collective-permute-start(f32[264,256]{1,0:T(8,128)S(1)} %get-tuple-element.107.own), channel_id=1, source_target_pairs={{0,64},{16,80},{32,96},{48,112},{64,0},{80,16},{96,32},{112,48},{1... | collective-permute-start | bytes 811016 | tf_op jit(solution)/shard_map/hop_0/ppermute | solution.py:476
  62.3 7.5 %collective-permute-start.12 = (f32[264,256]{1,0:T(8,128)S(1)}, f32[264,256]{1,0:T(8,128)S(1)}, u32[]{:S(2)}, u32[]{:S(2)}) collective-permute-start(f32[264,256]{1,0:T(8,128)S(1)} %total.11.group_map), channel_id=1, source_target_pairs={{8,12},{9,13},{10,14},{11,15},{24,28},{25,29},{26,30},{27,31},{40,... | collective-permute-start | bytes 811016 | tf_op jit(solution)/shard_map/hop_1/ppermute | solution.py:569
  63.2 6.6 %collective-permute-start.10 = (f32[8,256]{1,0:T(8,128)S(1)}, f32[8,256]{1,0:T(8,128)S(1)}, u32[]{:S(2)}, u32[]{:S(2)}) collective-permute-start(f32[8,256]{1,0:T(8,128)S(1)} %hop.3), channel_id=1, source_target_pairs={{4,14},{5,15},{6,12},{7,13},{20,30},{21,31},{22,28},{23,29},{36,46... | collective-permute-start | bytes 24584 | tf_op jit(solution)/shard_map/hop_1/ppermute | solution.py:567
  63.9 5.9 %collective-permute-start.9 = (f32[8,256]{1,0:T(8,128)S(1)}, f32[8,256]{1,0:T(8,128)S(1)}, u32[]{:S(2)}, u32[]{:S(2)}) collective-permute-start(f32[8,256]{1,0:T(8,128)S(1)} %hop.3), channel_id=1, source_target_pairs={{4,8},{5,9},{6,10},{7,11},{20,24},{21,25},{22,26},{23,27},{36,40},... | collective-permute-start | bytes 24584 | tf_op jit(solution)/shard_map/hop_1/ppermute | solution.py:566
  70.7 3.7 %collective-permute-start.13 = (f32[8,256]{1,0:T(8,128)S(1)}, f32[8,256]{1,0:T(8,128)S(1)}, u32[]{:S(2)}, u32[]{:S(2)}) collective-permute-start(f32[8,256]{1,0:T(8,128)S(1)} %get-tuple-element.122.own), channel_id=1, source_target_pairs={{0,192},{16,208},{32,224},{48,240},{64,128},{80,144},{96,160},{112... | collective-permute-start | bytes 24584 | tf_op jit(solution)/shard_map/spread_x/ppermute | solution.py:476
  74.6 4.2 %collective-permute-start.14 = (f32[8,256]{1,0:T(8,128)S(1)}, f32[8,256]{1,0:T(8,128)S(1)}, u32[]{:S(2)}, u32[]{:S(2)}) collective-permute-start(f32[8,256]{1,0:T(8,128)S(1)} %spread.4.own), channel_id=1, source_target_pairs={{0,1},{1,0},{2,3},{3,2},{4,5},{5,4},{6,7},{7,6},{8,9},{9,8},{10,11... | collective-permute-start | bytes 24584 | tf_op jit(solution)/shard_map/spread_core/ppermute | solution.py:476
  79.0 3.5 %collective-permute-start.15 = (f32[8,256]{1,0:T(8,128)S(1)}, f32[8,256]{1,0:T(8,128)S(1)}, u32[]{:S(2)}, u32[]{:S(2)}) collective-permute-start(f32[8,256]{1,0:T(8,128)S(1)} %spread.5.own), channel_id=1, source_target_pairs={{0,2},{1,3},{2,0},{3,1},{4,6},{5,7},{6,4},{7,5},{8,10},{9,11},{10,... | collective-permute-start | bytes 24584 | tf_op jit(solution)/shard_map/spread_z0/ppermute | solution.py:476
  82.8 7.1 %collective-permute-start.16 = (f32[8,256]{1,0:T(8,128)S(1)}, f32[8,256]{1,0:T(8,128)S(1)}, u32[]{:S(2)}, u32[]{:S(2)}) collective-permute-start(f32[8,256]{1,0:T(8,128)S(1)} %spread.6.own), channel_id=1, source_target_pairs={{0,4},{1,5},{2,6},{3,7},{4,0},{5,1},{6,2},{7,3},{8,12},{9,13},{10,... | collective-permute-start | bytes 24584 | tf_op jit(solution)/shard_map/spread_z1/ppermute | solution.py:476
  89.9 6.7 %copy-start.1 = (f32[16,256]{1,0:T(8,128)S(1)}, f32[16,256]{1,0:T(8,128)}, u32[]{:S(2)}) copy-start(f32[16,256]{1,0:T(8,128)} %get-tuple-element.76.filt) | copy-start | bytes 49156
  90.1 7.7 %collective-permute-start.17 = (f32[8,256]{1,0:T(8,128)S(1)}, f32[8,256]{1,0:T(8,128)S(1)}, u32[]{:S(2)}, u32[]{:S(2)}) collective-permute-start(f32[8,256]{1,0:T(8,128)S(1)} %spread.7), channel_id=1, source_target_pairs={{0,12},{1,13},{2,14},{3,15},{4,8},{5,9},{6,10},{7,11},{8,4},{9,5},... | collective-permute-start | bytes 24584 | tf_op jit(solution)/shard_map/spread_z2/ppermute | solution.py:476
